TPU v7x, 512 devices: a whole 4x4x16 slice. The times are simulated.
512 devices in a mesh: seq: 64 (over x, z), head: 8 (over y, core).
Axes of the slice: x: 4, y: 4, z: 16, core: 2. Of those that a mesh axis runs over, the one named last changes fastest.
Arguments:
- queries: bfloat16 [45056, 4096], P(('seq', 'head')), may hold values from -64 to 64
- database_rows: bfloat16 [512, 64, 896], P('seq', 'head'), may hold values from -6 to 6
- w_encoder: bfloat16 [896, 896], P('seq'), may hold values from -0.1875 to 0.1875
- w_key: bfloat16 [896, 4096], P(None, 'head'), may hold values from -0.1875 to 0.1875
- w_value: bfloat16 [896, 4096], P(None, 'head'), may hold values from -0.1875 to 0.1875
- neighbour_ids: int32 [704, 2], replicated, may hold values from 0 to 511, as said below
Outputs:
- attended: bfloat16 [45056, 4096], P(('seq', 'head'))
Inputs may be any that keep to these rules, and one draw needn't show every extreme that they name: `neighbour_ids`: among the 22 neighbours of the spans of one sequence shard (rows s * 11 onward), at most 2 are entries of any one database shard, and in every shard some database shard holds exactly 2 of them. The same entry may appear more than once.
All inputs are finite; a program needn't handle non-finite values.
Results may differ from a plain program's by a relative error of at most 0.012.
The roundings to bfloat16 on the way count: a program that leaves them out, or rounds other values in their place, can miss the bound.
Values may be sent and summed in bfloat16 or wider, within the bound.
A program may use at most 64 MiB of HBM per device.

v0:
```python
import jax
import jax.numpy as jnp
from jax import lax
from jax.sharding import Mesh
from jax.sharding import PartitionSpec as P

HEAD_DIM = 128
SPAN = 64
NBR_LEN = 64
K_NBR = 2
DB_DEV = 8
SEQ = ("seq_0", "seq_1")
HEAD = ("head_0", "head_1")
SEQ_HEAD = ("seq_0", "seq_1", "head_0", "head_1")


def joined_along(parts, dim):
    parts = jnp.moveaxis(parts, 0, dim)
    dims = parts.shape
    return parts.reshape(*dims[:dim], dims[dim] * dims[dim + 1], *dims[dim + 2 :])


def gather_in_order(shard, axes, order):
    parts = shard
    for k in order:
        parts = lax.all_gather(parts, axes[k])
    done = order[::-1]
    back = [done.index(k) for k in range(len(axes))]
    parts = parts.transpose(*back, *range(len(axes), parts.ndim))
    return parts.reshape(-1, *shard.shape)


def whole_of(shard, axes, order, dim):
    return joined_along(gather_in_order(shard, axes, order), dim)


def cut_rows(length, count):
    hop = length // count
    if hop >= 8:
        hop -= hop % 8
    return [hop * k for k in range(1, count)]


def gather_all_axes(shard, axes, dim):
    split_at = max(range(max(1, shard.ndim - 1)), key=lambda d: shard.shape[d])
    count, done = (len(axes), [])
    for initial, share in enumerate(
        jnp.split(shard, cut_rows(shard.shape[split_at], count), axis=split_at)
    ):
        if share.size:
            order = [(initial - k) % count for k in range(count)]
            done.append(gather_in_order(share, axes, order))
    return joined_along(jnp.concatenate(done, axis=split_at + 1), dim)


def encode_rows(raw_rows, w_encoder):
    values_in = raw_rows.astype(jnp.float32)
    mean_square = jnp.mean(values_in * values_in, axis=-1, keepdims=True)
    normed = (values_in * lax.rsqrt(mean_square + 1e-06)).astype(jnp.bfloat16)
    flat_normed = normed.reshape(-1, normed.shape[-1])
    summed = jnp.dot(
        flat_normed, whole_of(w_encoder, SEQ, (0, 1), 0), preferred_element_type=jnp.float32
    )
    return (values_in + jax.nn.silu(summed.reshape(values_in.shape))).astype(jnp.bfloat16)


def attend_spans(query_rows, keys, values):
    heads_here = query_rows.shape[1] // HEAD_DIM
    span_count = query_rows.shape[0] // SPAN
    query_block = query_rows.reshape(span_count, SPAN, heads_here, HEAD_DIM)
    key_block = keys.reshape(span_count, K_NBR * NBR_LEN, heads_here, HEAD_DIM)
    value_block = values.reshape(span_count, K_NBR * NBR_LEN, heads_here, HEAD_DIM)
    scores = jnp.einsum(
        "cqhd,ckhd->chqk", query_block, key_block, preferred_element_type=jnp.float32
    ) * HEAD_DIM ** (-0.5)
    highest = jnp.max(scores, axis=-1, keepdims=True)
    weights = jnp.exp(scores - highest)
    probs = (weights / jnp.sum(weights, axis=-1, keepdims=True)).astype(jnp.bfloat16)
    mixed = jnp.einsum("chqk,ckhd->cqhd", probs, value_block, preferred_element_type=jnp.float32)
    return mixed.astype(jnp.bfloat16).reshape(query_rows.shape)


def per_device(queries, database_rows, w_encoder, w_key, w_value, neighbour_ids):
    seq_count = lax.axis_size(SEQ)
    seq_index = lax.axis_index(SEQ)
    head_rows = lax.all_to_all(queries, HEAD, split_axis=1, concat_axis=0, tiled=True)
    encoded = encode_rows(database_rows, w_encoder)
    by_shard = neighbour_ids.reshape(seq_count, -1)
    cited_count = by_shard.shape[1]
    cap_count = max(2, (cited_count + seq_count - 1) // seq_count)
    cited_ids = lax.dynamic_index_in_dim(by_shard, seq_index, 0, keepdims=False)
    owners = by_shard // DB_DEV
    local_entry = by_shard % DB_DEV
    position = jnp.arange(cited_count, dtype=jnp.int32)
    same_owner = (owners[:, :, None] == owners[:, None, :]) & (
        position[None, None, :] < position[None, :, None]
    )
    earlier = jnp.sum(same_owner.astype(jnp.int32), axis=2)
    owned_here = owners == seq_index
    slot_index = jnp.arange(cap_count, dtype=jnp.int32)
    matches = owned_here[:, None, :] & (earlier[:, None, :] == slot_index[None, :, None])
    source_entry = jnp.sum(jnp.where(matches, local_entry[:, None, :], 0), axis=2)
    slot_filled = jnp.any(matches, axis=2)
    outgoing = jnp.where(
        slot_filled[:, :, None, None], encoded[source_entry], jnp.zeros((), jnp.bfloat16)
    )
    arrived = lax.all_to_all(outgoing, SEQ, split_axis=0, concat_axis=0, tiled=True)
    cited_owner = cited_ids // DB_DEV
    cited_slot = lax.dynamic_index_in_dim(earlier, seq_index, 0, keepdims=False)
    flat_arrived = arrived.reshape(-1, arrived.shape[2], arrived.shape[3])
    neighbours = flat_arrived[cited_owner * cap_count + cited_slot]
    full_rows = gather_all_axes(neighbours, HEAD, 1)
    flat_rows = full_rows.reshape(-1, full_rows.shape[2])
    keys = jnp.dot(flat_rows, w_key, preferred_element_type=jnp.float32).astype(jnp.bfloat16)
    values = jnp.dot(flat_rows, w_value, preferred_element_type=jnp.float32).astype(jnp.bfloat16)
    mixed = attend_spans(head_rows, keys, values)
    return lax.all_to_all(mixed, HEAD, split_axis=0, concat_axis=1, tiled=True)


def solution(mesh):
    torus = Mesh(mesh.devices.reshape(4, 16, 4, 2), ("seq_0", "seq_1", "head_0", "head_1"))
    in_specs = (
        P(SEQ_HEAD, None),
        P(SEQ, HEAD, None),
        P(SEQ, None),
        P(None, HEAD),
        P(None, HEAD),
        P(),
    )
    out_specs = P(SEQ_HEAD, None)
    return jax.shard_map(
        per_device, mesh=torus, in_specs=in_specs, out_specs=out_specs, check_vma=False
    )
```

profile of v0, /device:TPU:1, one launch (start us, length us, event | category | flops | bytes accessed | tf_op | source)
XLA Modules:
  0.0 275.8 jit_solution(14907422227870728838)
XLA Ops:
  6.5 12.5 %all-gather.6 = bf16[4,14,896]{2,1,0:T(8,128)(2,1)} all-gather(bf16[1,14,896]{2,1,0:T(8,128)(2,1)} %bitcast.69), channel_id=2, replica_groups=mesh['seq_0'=4,'seq_1'=16,'head_0'=4,'head_1'=2] {'seq_0'}, dimensions={0}, use_global_device_ids=true | all-gather | bytes 125440 | tf_op jit(solution)/shard_map/all_gather | solution.py:26
  20.9 1.0 fusion.15
  21.9 65.6 %all-gather.10.cloned.1.call-done = bf16[64,14,896]{2,1,0:T(8,128)(2,1)} async-done(((bf16[4,14,896]{2,1,0:T(8,128)(2,1)}), bf16[64,14,896]{2,1,0:T(8,128)(2,1)}) %all-gather.10.cloned.1.call-update) | async-done | bytes 1605648 | tf_op jit(solution)/shard_map/all_gather | solution.py:26
  87.5 1.6 copy.123
  89.2 1.4 reshape.287
  90.6 1.8 fusion.17
  93.3 1.6 broadcast_select_fusion
  94.9 9.9 %all-to-all-start = ((bf16[64,2,8,896]{3,2,1,0:T(8,128)(2,1)}), bf16[64,2,8,896]{3,2,1,0:T(8,128)(2,1)S(1)}, u32[]{:S(2)}, u32[]{:S(2)}) async-start(bf16[64,2,8,896]{3,2,1,0:T(8,128)(2,1)} %broadcast_select_fusion), calls=%async_computation | async-start | bytes 3670016 | tf_op jit(solution)/shard_map/all_to_all | solution.py:107
  105.0 71.2 %all-to-all-done = bf16[64,2,8,896]{3,2,1,0:T(8,128)(2,1)S(1)} async-done(((bf16[64,2,8,896]{3,2,1,0:T(8,128)(2,1)}), bf16[64,2,8,896]{3,2,1,0:T(8,128)(2,1)S(1)}, u32[]{:S(2)}, u32[]{:S(2)}) %all-to-all-start) | async-done | bytes 1835040 | tf_op jit(solution)/shard_map/all_to_all | solution.py:107
  176.9 17.2 %all-gather.4 = bf16[28,8,896]{2,1,0:T(8,128)(2,1)} all-gather(bf16[14,8,896]{2,1,0:T(8,128)(2,1)S(1)} %split.9), channel_id=6, replica_groups=mesh['seq_0'=4,'seq_1'=16,'head_0'=4,'head_1'=2] {'head_1'}, dimensions={0}, use_global_device_ids=true | all-gather | bytes 602112 | tf_op jit(solution)/shard_map/all_gather | solution.py:26
  194.2 16.7 %all_to_all.40 = bf16[88,8,512]{2,0,1:T(8,128)(2,1)S(1)} all-to-all(bf16[88,8,512]{2,0,1:T(8,128)(2,1)S(1)} %bitcast.61), channel_id=1, replica_groups=mesh['seq_0'=4,'seq_1'=16,'head_0'=4,'head_1'=2] {'head_0','head_1'}, dimensions={1} | all-to-all | bytes 1441792 | tf_op jit(solution)/shard_map/all_to_all | solution.py:86
  211.1 13.1 %all-gather.2 = bf16[32,8,896]{2,1,0:T(8,128)(2,1)S(1)} all-gather(bf16[8,8,896]{2,1,0:T(8,128)(2,1)S(1)} %split.8), channel_id=4, replica_groups=mesh['seq_0'=4,'seq_1'=16,'head_0'=4,'head_1'=2] {'head_0'}, dimensions={0}, use_global_device_ids=true | all-gather | bytes 573440 | tf_op jit(solution)/shard_map/all_gather | solution.py:26
  224.2 5.5 %all-gather.3 = bf16[8,8,8,896]{3,2,1,0:T(8,128)(2,1)S(1)} all-gather(bf16[4,8,8,896]{3,2,1,0:T(8,128)(2,1)S(1)} %bitcast.66), channel_id=5, replica_groups=mesh['seq_0'=4,'seq_1'=16,'head_0'=4,'head_1'=2] {'head_1'}, dimensions={0}, use_global_device_ids=true | all-gather | bytes 1376256 | tf_op jit(solution)/shard_map/all_gather | solution.py:26
  229.8 1.7 pad_maximum_fusion
  231.9 1.5 copy-done.1
  233.4 1.7 convolution_convert_fusion.1
  235.0 1.3 reshape.257
  236.3 3.6 %convolution_convert_fusion = bf16[1408,512]{1,0:T(8,128)(2,1)S(1)} fusion(bf16[1408,896]{1,0:T(8,128)(2,1)} %bitcast.63, bf16[896,512]{1,0:T(8,128)(2,1)} %param.9), kind=kOutput, calls=%fused_computation.3 | convolution fusion | flops 1292566528 | bytes 4882432 | tf_op jit(solution)/shard_map/dot_general | solution.py:114
  239.9 1.3 reshape.258
  241.2 2.4 fusion.3
  244.5 7.2 %fusion.10 = bf16[11,64,4,128]{3,1,2,0:T(8,128)(2,1)} fusion(bf16[11,128,4,128]{3,2,1,0:T(4,128)(2,1)} %reshape.257, f32[11,4,64]{2,1,0:T(4,128)S(1)} %fusion.25, f32[11,4,64,128]{3,2,1,0:T(8,128)S(1)} %fusion.3), kind=kOutput, calls=%fused_computation.17 | convolution fusion | flops 93719424 | bytes 3615744 | tf_op jit(solution)/shard_map/chqk,ckhd->cqhd/dot_general | solution.py:79
  251.7 1.7 copy.105
  253.7 14.4 %all_to_all.41 = bf16[8,88,512]{2,1,0:T(8,128)(2,1)S(1)} all-to-all(bf16[8,88,512]{2,1,0:T(8,128)(2,1)S(1)} %all_to_all.33), channel_id=1, replica_groups=mesh['seq_0'=4,'seq_1'=16,'head_0'=4,'head_1'=2] {'head_0','head_1'}, dimensions={0} | all-to-all | bytes 1441792 | tf_op jit(solution)/shard_map/all_to_all | solution.py:117
  268.0 0.9 copy.110
  (40 shorter events, 5.3 us)
Async XLA Ops:
  6.5 226.8 %copy-start = (bf16[896,512]{1,0:T(8,128)(2,1)S(1)}, bf16[896,512]{1,0:T(8,128)(2,1)}, u32[]{:S(2)}) copy-start(bf16[896,512]{1,0:T(8,128)(2,1)} %param.10) | copy-start | bytes 2752516
  6.5 81.0 %all-gather.10.cloned.1.call-start = ((), (), s32[]{:S(2)}) async-start(), calls=%async_computation.3 | async-start | bytes 1949696 | tf_op jit(solution)/shard_map/all_gather | solution.py:26
  89.2 1.4 copy-start.3
  94.9 81.4 %all-to-all-start = ((bf16[64,2,8,896]{3,2,1,0:T(8,128)(2,1)}), bf16[64,2,8,896]{3,2,1,0:T(8,128)(2,1)S(1)}, u32[]{:S(2)}, u32[]{:S(2)}) async-start(bf16[64,2,8,896]{3,2,1,0:T(8,128)(2,1)} %broadcast_select_fusion), calls=%async_computation | async-start | bytes 3670016 | tf_op jit(solution)/shard_map/all_to_all | solution.py:107
  104.8 125.1 %all-gather.12.cloned.1.call-start = ((), (), s32[]{:S(2)}) async-start(), calls=%async_computation.4 | async-start | bytes 2007040 | tf_op jit(solution)/shard_map/all_gather | solution.py:26
  176.9 17.2 %copy-start.2 = (bf16[88,4096]{1,0:T(8,128)(2,1)S(1)}, bf16[88,4096]{1,0:T(8,128)(2,1)}, u32[]{:S(2)}) copy-start(bf16[88,4096]{1,0:T(8,128)(2,1)} %param.6) | copy-start | bytes 2162692
  231.9 1.5 copy-start.1
Sparse Core Ops, SparseCore 0:
  19.2 68.2 all-gather.9
  194.2 32.6 all-gather.11
where the time goes:
time: 277 us; the launch traced here: 276 us
  waiting for transfers between devices  137 us (49%)
  blocking collectives  79.4 us (29%)
  matrix products  16.7 us (6%)
  local copies, waits for them, and re-layouts  13.8 us (5%)
  between operations  13.6 us (5%)
  starting transfers between devices  9.94 us (4%)
  other arithmetic  5.4 us (2%)
    all_to_all x1, waiting for transfers between devices, per_device(): lax.all_to_all(outgoing, SEQ, split_axis=0, concat_axis=0, tiled=True)  71.2 us
    all_gather x2, waiting for transfers between devices, gather_in_order(): parts = lax.all_gather(parts, axes[k])  65.6 us
    all_gather x4, blocking collectives, gather_in_order(): parts = lax.all_gather(parts, axes[k])  48.4 us
    all_to_all x1, blocking collectives, per_device(): lax.all_to_all(queries, HEAD, split_axis=1, concat_axis=0, tiled=True)  16.7 us
    all_to_all x1, blocking collectives, per_device(): return lax.all_to_all(mixed, HEAD, split_axis=0, concat_axis=1, tiled=True)  14.4 us
    all_to_all x1, starting transfers between devices, per_device(): lax.all_to_all(outgoing, SEQ, split_axis=0, concat_axis=0, tiled=True)  9.89 us
    dot_general x1, matrix products, attend_spans(): jnp.einsum('chqk,ckhd->cqhd', probs, value_block, preferred_element_type=...  7.18 us
  transfers between devices with their start and end apart: 3, of which 2 were waited for; matrix products, arithmetic and copies ran while one was open for 1% of the time, Pallas kernels for 0%

commit v1 on v0

v1 whole, which is shorter than its diff:
```python
import functools

import jax
import jax.numpy as jnp
from jax import lax
from jax.experimental import pallas as pl
from jax.experimental.pallas import tpu as pltpu
from jax.sharding import Mesh
from jax.sharding import PartitionSpec as P

HEAD_DIM = 128
SPAN = 64
NX, NZ, NY, NC = 4, 16, 4, 2
SEQ = ("x", "z")
HEAD = ("y", "c")
SEQ_HEAD = ("x", "z", "y", "c")
MESH = pl.DeviceIdType.MESH
BF16 = jnp.bfloat16
F32 = jnp.float32

ENC = 896
ENTRIES = 8
TOK = 8
SLOTS = 22
SUB = 4
WROWS = 14
COLS = 512
ROWS = 88
CHUNKS = 8
TILES = 8
GROUPS = ((0, 11),)


def kernel(
    tab_ref, db_ref, wsh_ref, q_ref, wk_ref, wv_ref, out_ref,
    zbuf, wz, wenc, wk, wv, qbuf, s_a, s_b, s_c, r_a, r_b, r_c, nb, enc, kbuf, vbuf, obuf,
    z_send, z_recv, wz_send, wz_recv, local, q_send, q_recv,
    wx_send, wx_recv, wy_send, wy_recv, wy_sib, x_send, x_recv,
    y_send, y_recv, y_sib, o_send, o_recv,
):
    x, z, y, c = (lax.axis_index(a) for a in ("x", "z", "y", "c"))
    r = 1 - 2 * c
    h = 2 * y + c

    def wrap(v, n):
        return lax.rem(v + 2 * n, n)

    def copy(src, dst, ssem, rsem, dev):
        return pltpu.make_async_remote_copy(
            src_ref=src, dst_ref=dst, send_sem=ssem, recv_sem=rsem,
            device_id=dev, device_id_type=MESH,
        )

    here = (x, z, y, c)
    sibling = (x, z, y, 1 - c)

    def at_x(dx):
        return (wrap(x + dx, NX), z, y, c)

    def at_z(dz):
        return (x, wrap(z + dz, NZ), y, c)

    def at_y(dy):
        return (x, z, wrap(y + dy, NY), c)

    others = [(0, 1)] + [(dy, e) for dy in (2, 1, 3) for e in (0, 1)]

    def at_head(dy, e):
        return (x, z, wrap(y + dy, NY), wrap(c + e, NC))

    barrier = pltpu.get_barrier_semaphore()
    partners = [at_z(1), at_z(-1), at_x(1), at_x(2), at_x(3)] + [at_head(*o) for o in others]
    for dev in partners:
        pl.semaphore_signal(barrier, inc=1, device_id=dev, device_id_type=MESH)
    pl.semaphore_wait(barrier, len(partners))

    def zpiece(owner, i):
        return zbuf.at[pl.ds(owner * ENTRIES + i * (ENTRIES // SUB), ENTRIES // SUB)]

    sends = []

    def go(cp):
        cp.start()
        sends.append(cp)

    for d in range(2):
        dev = at_z(r if d == 0 else -r)
        go(copy(wsh_ref.at[h], wz.at[x, z], wz_send.at[d, 0], wz_recv.at[d, 0], dev))
    for i in range(SUB):
        for d in range(2):
            dev = at_z(r if d == 0 else -r)
            go(copy(
                db_ref.at[pl.ds(i * (ENTRIES // SUB), ENTRIES // SUB)], zpiece(z, i),
                z_send.at[d, 0, i], z_recv.at[d, 0, i], dev,
            ))

    for n, (dy, e) in enumerate(others):
        dev = at_head(dy, e)
        to = 2 * dev[2] + dev[3]
        cols = pl.ds(pl.multiple_of(to * COLS, COLS), COLS)
        go(copy(q_ref.at[:, cols], qbuf.at[h], q_send.at[n], q_recv.at[h], dev))

    own_cols = pl.ds(pl.multiple_of(h * COLS, COLS), COLS)
    locals_ = [
        pltpu.make_async_copy(db_ref, zbuf.at[pl.ds(z * ENTRIES, ENTRIES)], local.at[0]),
        pltpu.make_async_copy(wsh_ref.at[h], wz.at[x, z], local.at[1]),
        pltpu.make_async_copy(wk_ref, wk, local.at[2]),
        pltpu.make_async_copy(wv_ref, wv, local.at[3]),
        pltpu.make_async_copy(q_ref.at[:, own_cols], qbuf.at[h], local.at[4]),
    ]
    for cp in locals_:
        cp.start()

    def z_arrive(d, k, forward):
        way = r if d == 0 else -r
        owner = wrap(z - way * (1 + k), NZ)
        dev = at_z(way)
        piece = wz.at[x, owner]
        copy(piece, piece, wz_send.at[d, k], wz_recv.at[d, k], dev).wait_recv()
        if forward:
            copy(piece, piece, wz_send.at[d, k + 1], wz_recv.at[d, k + 1], dev).start()

        def part(i):
            piece = zpiece(owner, i)
            copy(piece, piece, z_send.at[d, k, i], z_recv.at[d, k, i], dev).wait_recv()
            if forward:
                copy(piece, piece, z_send.at[d, k + 1, i], z_recv.at[d, k + 1, i], dev).start()

        return part

    def z_step(k, forwards):
        parts = [z_arrive(d, k, f) for d, f in forwards]
        for i in range(SUB):
            for part in parts:
                part(i)

    hops = (NZ // 2, NZ // 2 - 1)

    @pl.loop(0, hops[1] - 1)
    def _(k):
        z_step(k, ((0, True), (1, True)))

    z_step(hops[1] - 1, ((0, True), (1, False)))
    z_step(hops[0] - 1, ((0, False),))

    locals_[0].wait()
    locals_[1].wait()

    for n in range(1, NX):
        go(copy(wz.at[x], wz.at[x], wx_send.at[n], wx_recv.at[x], at_x(n)))

    def entry(dest, j):
        n = tab_ref[dest, j]
        return zbuf[n & (NZ * ENTRIES - 1)], n >> 7

    def slots(g):
        return range(2 * GROUPS[g][0], 2 * GROUPS[g][1])

    def slot_ds(g):
        a, b = GROUPS[g]
        return pl.ds(2 * a, 2 * (b - a))

    n_groups = len(GROUPS)
    far, near = wrap(x + 2 * r, NX), wrap(x - r, NX)
    ahead = wrap(x + r, NX)
    for g in range(n_groups):
        for j in slots(g):
            s_a[j] = entry(far, j)[0]
        go(copy(s_a.at[slot_ds(g)], r_a.at[slot_ds(g)], x_send.at[0, g], x_recv.at[0, g], at_x(r)))
        for j in slots(g):
            s_b[j] = entry(near, j)[0]
        go(copy(s_b.at[slot_ds(g)], r_b.at[slot_ds(g)], x_send.at[1, g], x_recv.at[1, g], at_x(-r)))

    for n in range(1, NX):
        src = wrap(x + n, NX)
        copy(wz.at[src], wz.at[src], wx_send.at[n], wx_recv.at[src], at_x(n)).wait_recv()
    lhs_rows, rhs_rows = ENTRIES * WROWS, ENTRIES * 16
    row = lax.broadcasted_iota(jnp.int32, (lhs_rows, rhs_rows), 0)
    col = lax.broadcasted_iota(jnp.int32, (lhs_rows, rhs_rows), 1)
    inner = col & 15
    pick = jnp.where((inner < WROWS) & ((col >> 4) * WROWS + inner == row), 1.0, 0.0).astype(BF16)
    for a in range(NX):
        for b in range(2):
            block = wz[a, pl.ds(b * ENTRIES, ENTRIES)].reshape(rhs_rows, 128)
            packed = jnp.dot(pick, block, preferred_element_type=F32).astype(BF16)
            wenc[h, pl.ds((2 * a + b) * lhs_rows, lhs_rows), :] = packed

    class Gather:
        def __init__(self, region, send, recv, sib):
            self.region, self.send, self.recv, self.sib = region, send, recv, sib

        def start(self):
            own = self.region(h)
            go(copy(own, own, self.send(0), self.recv(0), at_y(r)))
            go(copy(own, own, self.send(1), self.recv(1), at_y(-r)))
            go(copy(own, own, self.send(2), self.sib(0), sibling))

        def arrive(self, n):
            step = (-1, 1, 2)[n] * r
            src = wrap(y + step, NY)
            piece = self.region(2 * src + c)
            copy(piece, piece, self.send(0), self.recv(n), at_y(r)).wait_recv()
            if n == 0:
                go(copy(piece, piece, self.send(3), self.recv(2), at_y(r)))
            go(copy(piece, piece, self.send(4 + n), self.sib(wrap(step, NY)), sibling))

        def from_sibling(self, delta):
            src = wrap(y + delta, NY)
            piece = self.region(2 * src + 1 - c)
            copy(piece, piece, self.send(0), self.sib(delta), sibling).wait_recv()

    w_gather = Gather(
        lambda t: wenc.at[t], lambda n: wy_send.at[n], lambda n: wy_recv.at[n], lambda n: wy_sib.at[n]
    )
    w_gather.start()

    for g in range(n_groups):
        copy(s_a.at[slot_ds(g)], r_a.at[slot_ds(g)], x_send.at[0, g], x_recv.at[0, g], at_x(r)).wait_recv()
        for j in slots(g):
            mine, col_of = entry(ahead, j)
            s_c[j] = jnp.where(col_of == x, mine, r_a[j])
        go(copy(s_c.at[slot_ds(g)], r_c.at[slot_ds(g)], x_send.at[2, g], x_recv.at[2, g], at_x(r)))

    for n in range(3):
        w_gather.arrive(n)
    for n in range(NY):
        w_gather.from_sibling(n)

    gathers = []
    for g in range(n_groups):
        a, b = GROUPS[g]
        count = 2 * (b - a)
        rows = pl.ds(16 * a, 16 * (b - a))
        copy(s_b.at[slot_ds(g)], r_b.at[slot_ds(g)], x_send.at[1, g], x_recv.at[1, g], at_x(-r)).wait_recv()
        copy(s_c.at[slot_ds(g)], r_c.at[slot_ds(g)], x_send.at[2, g], x_recv.at[2, g], at_x(r)).wait_recv()
        for j in slots(g):
            mine, col_of = entry(x, j)
            nb[j] = jnp.where(col_of == x, mine, jnp.where(col_of == ahead, r_b[j], r_c[j]))
        raw = nb[2 * a : 2 * b].astype(F32).reshape(count * TOK, ENC)
        mean_square = jnp.sum(raw * raw, axis=-1, keepdims=True) * (1.0 / ENC)
        normed = (raw * lax.rsqrt(mean_square + 1e-06)).astype(BF16)
        for t in range(TILES // 2):
            w2 = jnp.concatenate([wenc[2 * t], wenc[2 * t + 1]], axis=1)
            summed = jnp.dot(normed, w2, preferred_element_type=F32)
            width = min(256, ENC - 256 * t)
            summed = summed[:, :width]
            part = raw[:, 256 * t : 256 * t + width]
            enc[h, rows, 256 * t : 256 * t + width] = (part + summed * jax.nn.sigmoid(summed)).astype(BF16)
        gather = Gather(
            lambda t, rows=rows: enc.at[t, rows],
            lambda n, g=g: y_send.at[g, n],
            lambda n, g=g: y_recv.at[g, n],
            lambda n, g=g: y_sib.at[g, n],
        )
        gather.start()
        gathers.append(gather)

    locals_[2].wait()
    locals_[3].wait()

    def project(g, chip):
        a, b = GROUPS[g]
        n = 16 * (b - a)
        rows = pl.ds(16 * a, n)
        pair = pl.ds(2 * chip, 2)
        lhs = enc[pair, rows, :].reshape(2 * n, ENC)
        for w, out in ((wk, kbuf), (wv, vbuf)):
            got = jnp.dot(lhs, w[...], preferred_element_type=F32).astype(BF16)
            out[pair, rows, :] = got.reshape(2, n, COLS)

    for g in range(n_groups):
        gathers[g].from_sibling(0)
        project(g, y)
        gathers[g].arrive(0)
        gathers[g].arrive(1)
        for dy in (1, 3):
            gathers[g].from_sibling(dy)
            project(g, wrap(y + dy, NY))
        gathers[g].arrive(2)
        gathers[g].from_sibling(2)
        project(g, wrap(y + 2, NY))

    locals_[4].wait()
    for n, (dy, e) in enumerate(others):
        src = 2 * wrap(y + dy, NY) + wrap(c + e, NC)
        copy(qbuf.at[src], qbuf.at[src], q_send.at[n], q_recv.at[src], sibling).wait_recv()

    def attend(chunk):
        first = lax.div(11 * chunk, 8) - lax.div(chunk, 7)
        token = lax.broadcasted_iota(jnp.int32, (ROWS, 128), 0) + ROWS * chunk
        span_of = token >> 6
        for hd in range(COLS // HEAD_DIM):
            cols = slice(hd * HEAD_DIM, (hd + 1) * HEAD_DIM)

            def window(ref):
                spans = []
                for s in range(3):
                    rows = pl.ds(pl.multiple_of(16 * (first + s), 16), 16)
                    spans.append(ref[:, rows, cols].reshape(128, HEAD_DIM))
                return jnp.concatenate(spans, axis=0)

            scores = lax.dot_general(
                qbuf[chunk, :, cols], window(kbuf), (((1,), (1,)), ((), ())),
                preferred_element_type=F32,
            ) * HEAD_DIM ** (-0.5)
            parts = [
                jnp.where(span_of == first + s, scores[:, 128 * s : 128 * s + 128], -1e30) for s in range(3)
            ]
            highest = jnp.max(jnp.maximum(jnp.maximum(parts[0], parts[1]), parts[2]), axis=-1, keepdims=True)
            weights = [jnp.exp(p - highest) for p in parts]
            total = jnp.sum(weights[0] + weights[1] + weights[2], axis=-1, keepdims=True)
            probs = jnp.concatenate([(w / total).astype(BF16) for w in weights], axis=1)
            mixed = jnp.dot(probs, window(vbuf), preferred_element_type=F32)
            obuf[chunk, :, cols] = mixed.astype(BF16)

    for n, (dy, e) in enumerate(others[1:] + others[:1]):
        dev = at_head(dy, e)
        chunk = 2 * dev[2] + dev[3]
        attend(chunk)
        go(copy(obuf.at[chunk], out_ref.at[:, own_cols], o_send.at[n], o_recv.at[h], dev))
    attend(h)
    own_out = pltpu.make_async_copy(obuf.at[h], out_ref.at[:, own_cols], local.at[5])
    own_out.start()
    own_out.wait()
    for dy, e in others:
        src = 2 * wrap(y + dy, NY) + wrap(c + e, NC)
        cols = pl.ds(pl.multiple_of(src * COLS, COLS), COLS)
        dst = out_ref.at[:, cols]
        copy(obuf.at[h], dst, o_send.at[0], o_recv.at[src], sibling).wait_recv()

    for cp in sends:
        cp.wait_send()

    def z_sent(d, k):
        dev = at_z(r)
        piece = wz.at[x, z]
        copy(piece, piece, wz_send.at[d, k], wz_recv.at[d, k], dev).wait_send()
        for i in range(SUB):
            piece = zpiece(z, i)
            copy(piece, piece, z_send.at[d, k, i], z_recv.at[d, k, i], dev).wait_send()

    @pl.loop(1, hops[1])
    def _(k):
        for d in range(2):
            z_sent(d, k)

    z_sent(0, hops[0] - 1)


def per_device(queries, database_rows, w_encoder, w_key, w_value, neighbour_ids):
    z = lax.axis_index("z")
    table = lax.dynamic_index_in_dim(neighbour_ids.reshape(NX, NZ, SLOTS), z, 1, keepdims=False)
    padded = jnp.pad(w_encoder, ((0, 16 - WROWS), (0, 128 * TILES - ENC)))
    tiles = padded.reshape(16, TILES, 128).transpose(1, 0, 2)
    g = len(GROUPS)
    dma = pltpu.SemaphoreType.DMA
    slots = pltpu.VMEM((SLOTS, TOK, ENC), BF16)
    any_ = pl.BlockSpec(memory_space=pl.ANY)
    return pl.pallas_call(
        kernel,
        out_shape=jax.ShapeDtypeStruct(queries.shape, BF16),
        in_specs=[pl.BlockSpec(memory_space=pltpu.SMEM)] + [any_] * 5,
        out_specs=any_,
        scratch_shapes=[
            pltpu.VMEM((NZ * ENTRIES, TOK, ENC), BF16),
            pltpu.VMEM((NX, NZ, 16, 128), BF16),
            pltpu.VMEM((TILES, ENC, 128), BF16),
            pltpu.VMEM((ENC, COLS), BF16),
            pltpu.VMEM((ENC, COLS), BF16),
            pltpu.VMEM((CHUNKS, ROWS, COLS), BF16),
            slots, slots, slots, slots, slots, slots, slots,
            pltpu.VMEM((CHUNKS, SLOTS * TOK, ENC), BF16),
            pltpu.VMEM((CHUNKS, SLOTS * TOK, COLS), BF16),
            pltpu.VMEM((CHUNKS, SLOTS * TOK, COLS), BF16),
            pltpu.VMEM((CHUNKS, ROWS, COLS), BF16),
            dma((2, NZ // 2, SUB)), dma((2, NZ // 2, SUB)),
            dma((2, NZ // 2)), dma((2, NZ // 2)),
            dma((6,)),
            dma((7,)), dma((CHUNKS,)),
            dma((NX,)), dma((NX,)),
            dma((7,)), dma((3,)), dma((NY,)),
            dma((3, g)), dma((3, g)),
            dma((g, 7)), dma((g, 3)), dma((g, NY)),
            dma((7,)), dma((CHUNKS,)),
        ],
        compiler_params=pltpu.CompilerParams(
            collective_id=0, has_side_effects=True, vmem_limit_bytes=48 * 1024 * 1024
        ),
        name="exchange_attend",
    )(table, database_rows, tiles, queries, w_key, w_value)


def solution(mesh):
    torus = Mesh(mesh.devices.reshape(NX, NZ, NY, NC), SEQ_HEAD)
    in_specs = (
        P(SEQ_HEAD, None), P(SEQ, HEAD, None), P(SEQ, None), P(None, HEAD), P(None, HEAD), P(),
    )
    return jax.shard_map(
        per_device, mesh=torus, in_specs=in_specs, out_specs=P(SEQ_HEAD, None), check_vma=False
    )
```

time: 277 us -> 97.4 us (0.35)
  waiting for transfers between devices: 137 us -> 0 us
  Pallas kernels: 0 us -> 91.4 us
  blocking collectives: 79.4 us -> 0 us
  matrix products: 16.7 us -> 0 us
  between operations: 13.6 us -> 0.05 us
  starting transfers between devices: 9.94 us -> 0 us
  local copies, waits for them, and re-layouts: 13.8 us -> 5.77 us
  other arithmetic: 5.4 us -> 0 us
    pallas_call x0 -> x1, Pallas kernels: none -> 91.4 us  [per_device(): pl.pallas_call(kernel, out_shape=jax.ShapeDtypeStruct(queries.shape, BF16...]
    all_to_all x1 -> x0, waiting for transfers between devices: 71.2 us -> none  [per_device(): lax.all_to_all(outgoing, SEQ, split_axis=0, concat_axis=0, tiled=True)]
    all_gather x2 -> x0, waiting for transfers between devices: 65.6 us -> none  [gather_in_order(): parts = lax.all_gather(parts, axes[k])]
    all_gather x4 -> x0, blocking collectives: 48.4 us -> none  [gather_in_order(): parts = lax.all_gather(parts, axes[k])]
    all_to_all x2 -> x0, blocking collectives: 31.1 us -> none  [the longest x1 16.7 us: per_device(): lax.all_to_all(queries, HEAD, split_axis=1, concat_axis=0, tiled=True)]
    dot_general x5 -> x0, matrix products: 16.7 us -> none  [the longest x1 7.18 us: attend_spans(): jnp.einsum('chqk,ckhd->cqhd', probs, value_block, preferred_element_type=...]
    all_to_all x1 -> x0, starting transfers between devices: 9.89 us -> none  [per_device(): lax.all_to_all(outgoing, SEQ, split_axis=0, concat_axis=0, tiled=True)]
    reshape x5 -> x1, local copies, waits for them, and re-layouts: 2.99 us -> 0.14 us  [per_device(): neighbour_ids.reshape(NX, NZ, SLOTS)]
  transfers between devices with their start and end apart: 3 -> 0, of which waited for: 2 -> 0; matrix products, arithmetic and copies ran while one was open for 1% -> 0% of each run, Pallas kernels for 0% -> 0%
where the time goes in v1:
time: 97.4 us; the launch traced here: 97.2 us
  Pallas kernels  91.4 us (94%)
  local copies, waits for them, and re-layouts  5.77 us (6%)
    pallas_call x1, Pallas kernels, per_device(): pl.pallas_call(kernel, out_shape=jax.ShapeDtypeStruct(queries.shape, BF16...  91.4 us
    unnamed x10, local copies, waits for them, and re-layouts  4.8 us

profile of v1, /device:TPU:1, one launch (start us, length us, event | category | flops | bytes accessed | tf_op | source)
XLA Modules:
  0.0 97.2 jit_solution(12542088328738848074)
XLA Ops:
  0.0 0.0 copy-start.2
  0.0 0.8 bitcast_bitcast_fusion.wsh_ref
  0.8 0.9 copy.7
  1.7 0.0 copy-start.3
  1.7 0.1 reshape.6
  1.9 0.0 copy-done.2
  1.9 0.7 copy-done.3
  2.6 0.0 copy-start
  2.6 1.2 %copy-done = bf16[896,512]{1,0:T(8,128)(2,1)S(1)} copy-done((bf16[896,512]{1,0:T(8,128)(2,1)S(1)}, bf16[896,512]{1,0:T(8,128)(2,1)}, u32[]{:S(2)}) %copy-start) | copy-done | bytes 917528
  3.8 0.0 copy-start.1
  3.8 1.2 %copy-done.1 = bf16[896,512]{1,0:T(8,128)(2,1)S(1)} copy-done((bf16[896,512]{1,0:T(8,128)(2,1)S(1)}, bf16[896,512]{1,0:T(8,128)(2,1)}, u32[]{:S(2)}) %copy-start.1) | copy-done | bytes 917528
  5.0 91.4 %exchange_attend.1 = bf16[88,4096]{1,0:T(8,128)(2,1)S(1)} custom-call(s32[4,22]{1,0:T(4,128)S(1)} %bitcast.8, bf16[8,8,896]{2,1,0:T(8,128)(2,1)S(1)} %copy-done.3, bf16[8,16,128]{2,1,0:T(8,128)(2,1)S(1)} %bitcast_bitcast_fusion.wsh_ref, bf16[88,4096]{1,0:T(8,128)(2,1)S(1)} %copy-done.2, bf16[896,512]{1,0:T(8,128)(2,1)S(1)} %copy-done, ...), custom_call_target="tpu_custom_call" | custom-call | tf_op jit(solution)/shard_map/exchange_attend/pallas_call | solution.py:359
  96.3 0.9 copy.12
  (1 shorter events, 0.0 us)
Async XLA Ops:
  0.0 1.9 %copy-start.2 = (bf16[88,4096]{1,0:T(8,128)(2,1)S(1)}, bf16[88,4096]{1,0:T(8,128)(2,1)}, u32[]{:S(2)}) copy-start(bf16[88,4096]{1,0:T(8,128)(2,1)} %q_ref.1) | copy-start | bytes 2162692
  1.7 0.9 copy-start.3
  2.6 1.2 %copy-start = (bf16[896,512]{1,0:T(8,128)(2,1)S(1)}, bf16[896,512]{1,0:T(8,128)(2,1)}, u32[]{:S(2)}) copy-start(bf16[896,512]{1,0:T(8,128)(2,1)} %wk_ref.1) | copy-start | bytes 2752516
  3.8 1.2 %copy-start.1 = (bf16[896,512]{1,0:T(8,128)(2,1)S(1)}, bf16[896,512]{1,0:T(8,128)(2,1)}, u32[]{:S(2)}) copy-start(bf16[896,512]{1,0:T(8,128)(2,1)} %wv_ref.1) | copy-start | bytes 2752516

commit v2 on v1

v2 whole, which is shorter than its diff:
```python
import jax
import jax.numpy as jnp
from jax import lax
from jax.experimental import pallas as pl
from jax.experimental.pallas import tpu as pltpu
from jax.sharding import Mesh
from jax.sharding import PartitionSpec as P

HEAD_DIM = 128
NX, NZ, NY, NC = 4, 16, 4, 2
SEQ = ("x", "z")
HEAD = ("y", "c")
SEQ_HEAD = ("x", "z", "y", "c")
MESH = pl.DeviceIdType.MESH
BF16 = jnp.bfloat16
F32 = jnp.float32

ENC = 896
ENTRIES = 8
TOK = 8
SLOTS = 22
CAP = 2
SUB = 4
WROWS = 14
COLS = 512
ROWS = 88
CHUNKS = 8
TILES = 8
LEAP = 4

GROUPS = ((0, 5), (5, 9), (9, 13), (13, 16))
READY = {1: 0, 3: 1, 5: 2, 7: 3}
PIECES = ((0, 6), (6, 11))


def order_of(d, way):
    return 2 * d - 1 + way


def kernel(
    ids_ref, db_ref, wsh_ref, q_ref, wk_ref, wv_ref, out_ref,
    vtab, inv_ref, own_ref, z0, z1, z2, z3, wz, wenc, wk, wv, qbuf, s_x, r_x, raw, enc, kbuf, vbuf, obuf,
    z_send, z_recv, wz_send, wz_recv, local, q_send, q_recv,
    wx_send, wx_recv, wy_send, wy_recv, wy_sib, x_send, x_recv,
    y_send, y_recv, e_send, e_recv, o_send, o_recv,
):
    x, z, y, c = (lax.axis_index(a) for a in SEQ_HEAD)
    r = 1 - 2 * c
    h = 2 * y + c
    zg = (z0, z1, z2, z3)

    def wrap(v, n):
        return lax.rem(v + 2 * n, n)

    def copy(src, dst, ssem, rsem, dev):
        return pltpu.make_async_remote_copy(
            src_ref=src, dst_ref=dst, send_sem=ssem, recv_sem=rsem,
            device_id=dev, device_id_type=MESH,
        )

    sibling = (x, z, y, 1 - c)

    def at_x(dx):
        return (wrap(x + dx, NX), z, y, c)

    def at_z(dz):
        return (x, wrap(z + dz, NZ), y, c)

    def at_y(dy):
        return (x, z, wrap(y + dy, NY), c)

    others = [(0, 1)] + [(dy, e) for dy in (2, 1, 3) for e in (0, 1)]

    def at_head(dy, e):
        return (x, z, wrap(y + dy, NY), wrap(c + e, NC))

    barrier = pltpu.get_barrier_semaphore()
    partners = [at_z(s * d) for d in range(1, LEAP + 1) for s in (1, -1)]
    partners += [at_x(n) for n in range(1, NX)] + [at_head(*o) for o in others]
    for dev in partners:
        pl.semaphore_signal(barrier, inc=1, device_id=dev, device_id_type=MESH)
    pl.semaphore_wait(barrier, len(partners))

    sends = []

    def go(cp):
        cp.start()
        sends.append(cp)

    def w_copy(n, slot, dist):
        return copy(wz.at[x, slot], wz.at[x, slot], wz_send.at[n], wz_recv.at[slot], at_z(r * dist))

    for n, d in enumerate([s * d for d in range(1, LEAP + 1) for s in (1, -1)]):
        slot = d % NZ
        go(copy(wsh_ref.at[h], wz.at[x, slot], wz_send.at[n], wz_recv.at[slot], at_z(r * d)))

    def zpiece(place, i):
        g = next(k for k, (a, b) in enumerate(GROUPS) if a <= place < b)
        n = ENTRIES // SUB
        return zg[g].at[pl.ds((place - GROUPS[g][0]) * ENTRIES + i * n, n)]

    def z_dev(way):
        return at_z(r if way == 0 else -r)

    for i in range(SUB):
        for way in range(2):
            go(copy(
                db_ref.at[pl.ds(i * (ENTRIES // SUB), ENTRIES // SUB)], zpiece(order_of(1, way), i),
                z_send.at[way, 0, i], z_recv.at[way, 0, i], z_dev(way),
            ))

    for n, (dy, e) in enumerate(others):
        dev = at_head(dy, e)
        to = 2 * dev[2] + dev[3]
        cols = pl.ds(pl.multiple_of(to * COLS, COLS), COLS)
        go(copy(q_ref.at[:, cols], qbuf.at[h], q_send.at[n], q_recv.at[h], dev))

    own_cols = pl.ds(pl.multiple_of(h * COLS, COLS), COLS)
    locals_ = [
        pltpu.make_async_copy(db_ref, z0.at[pl.ds(0, ENTRIES)], local.at[0]),
        pltpu.make_async_copy(wsh_ref.at[h], wz.at[x, 0], local.at[1]),
        pltpu.make_async_copy(wk_ref, wk, local.at[2]),
        pltpu.make_async_copy(wv_ref, wv, local.at[3]),
        pltpu.make_async_copy(q_ref.at[:, own_cols], qbuf.at[h], local.at[4]),
    ]
    for cp in locals_:
        cp.start()

    ids = ids_ref[...]
    lane = lax.broadcasted_iota(jnp.int32, (8, 128), 1)
    owner_of = ids >> 3
    number = jnp.zeros_like(ids)
    for k in range(1, SLOTS):
        same = (pltpu.roll(owner_of, k, 1) == owner_of) & (lane >= k)
        number = number + jnp.where(same, 1, 0)
    behind = (r * (z - (owner_of & (NZ - 1)))) & (NZ - 1)
    place_of = jnp.where(behind < NZ // 2, jnp.maximum(2 * behind - 1, 0), 2 * (NZ - behind))
    place_of = jnp.where(behind == NZ // 2, NZ - 1, place_of)
    slot_of = CAP * place_of + number
    column_of = owner_of >> 4
    key = jnp.where(column_of == x, slot_of * ENTRIES + (ids & (ENTRIES - 1)), -1)
    inverse = jnp.zeros_like(ids)
    for k in range(SLOTS):
        one = jnp.broadcast_to(key[:, k : k + 1], (8, 128))
        inverse = inverse + jnp.where((one >> 3) == lane, one & (ENTRIES - 1), 0)
    vtab[0] = inverse
    vtab[1] = slot_of * NX + column_of
    to_scalar = [
        pltpu.make_async_copy(vtab.at[0], inv_ref, local.at[6]),
        pltpu.make_async_copy(vtab.at[1], own_ref, local.at[7]),
    ]
    for cp in to_scalar:
        cp.start()

    def z_step(k):
        d = k + 1
        for i in range(SUB):
            for way in range(2):
                if d == NZ // 2 and way == 1:
                    continue
                piece = zpiece(order_of(d, way), i)
                copy(piece, piece, z_send.at[way, k, i], z_recv.at[way, k, i], z_dev(way)).wait_recv()
                if d + 1 < NZ // 2 or (d + 1 == NZ // 2 and way == 0):
                    go(copy(
                        piece, zpiece(order_of(d + 1, way), i),
                        z_send.at[way, k + 1, i], z_recv.at[way, k + 1, i], z_dev(way),
                    ))

    def w_arrived(slot):
        copy(wz.at[x, slot], wz.at[x, slot], wz_send.at[0], wz_recv.at[slot], at_z(1)).wait_recv()

    def w_leap():
        n = 2 * LEAP
        for s in (1, -1):
            held = s * LEAP % NZ
            w_arrived(held)
            for d in range(1, LEAP + 1):
                total = LEAP + d
                if total == NZ // 2 and s == -1:
                    continue
                slot = s * total % NZ
                go(copy(wz.at[x, held], wz.at[x, slot], wz_send.at[n], wz_recv.at[slot], at_z(s * r * d)))
                n += 1

    def w_columns():
        for slot in range(1, NZ):
            if slot not in (LEAP, NZ - LEAP):
                w_arrived(slot)
        locals_[1].wait()
        for n in range(1, NX):
            go(copy(wz.at[x], wz.at[x], wx_send.at[n], wx_recv.at[x], at_x(n)))

    class Gather:
        def start(self):
            own = wenc.at[h]
            go(copy(own, own, wy_send.at[0], wy_recv.at[0], at_y(r)))
            go(copy(own, own, wy_send.at[1], wy_recv.at[1], at_y(-r)))
            go(copy(own, own, wy_send.at[2], wy_sib.at[0], sibling))

        def arrive(self, n):
            step = (-1, 1, 2)[n] * r
            piece = wenc.at[2 * wrap(y + step, NY) + c]
            copy(piece, piece, wy_send.at[0], wy_recv.at[n], at_y(r)).wait_recv()
            if n == 0:
                go(copy(piece, piece, wy_send.at[3], wy_recv.at[2], at_y(r)))
            go(copy(piece, piece, wy_send.at[4 + n], wy_sib.at[wrap(step, NY)], sibling))

        def from_sibling(self, delta):
            piece = wenc.at[2 * wrap(y + delta, NY) + 1 - c]
            copy(piece, piece, wy_send.at[0], wy_sib.at[delta], sibling).wait_recv()

    w_gather = Gather()

    def w_pack():
        for n in range(1, NX):
            src = wrap(x + n, NX)
            copy(wz.at[src], wz.at[src], wx_send.at[n], wx_recv.at[src], at_x(n)).wait_recv()
        lhs_rows, rhs_rows = ENTRIES * WROWS, NZ * 16
        row = lax.broadcasted_iota(jnp.int32, (lhs_rows, rhs_rows), 0)
        col = lax.broadcasted_iota(jnp.int32, (lhs_rows, rhs_rows), 1)
        owner = (z - r * (col >> 4)) & (NZ - 1)
        inner = col & 15
        place = owner * WROWS + inner
        for b in range(2):
            pick = jnp.where((inner < WROWS) & (place == row + b * lhs_rows), 1.0, 0.0).astype(BF16)
            for a in range(NX):
                block = wz[a].reshape(rhs_rows, 128)
                packed = jnp.dot(pick, block, preferred_element_type=F32).astype(BF16)
                wenc[h, pl.ds((2 * a + b) * lhs_rows, lhs_rows), :] = packed
        w_gather.start()

    def x_slots(g):
        return CAP * GROUPS[g][0], CAP * (GROUPS[g][1] - GROUPS[g][0])

    def x_exchange(g):
        first, count = x_slots(g)
        for n in (2, 1, 3, 0):
            dest = wrap(x + n, NX)
            for j in range(first, first + count):
                at = (j // CAP - GROUPS[g][0]) * ENTRIES + (inv_ref[dest, j] & (ENTRIES - 1))
                if n:
                    s_x[n - 1, j] = zg[g][at]
                else:
                    r_x[x, j] = zg[g][at]
            if n:
                part = pl.ds(first, count)
                go(copy(s_x.at[n - 1, part], r_x.at[x, part], x_send.at[n, g], x_recv.at[x, g], at_x(n)))

    locals_[0].wait()
    for cp in to_scalar:
        cp.wait()
    for k in range(NZ // 2):
        z_step(k)
        if k == 0:
            w_leap()
        if k in READY:
            x_exchange(READY[k])
        if k == 2:
            w_columns()
        if k == 4:
            w_pack()
        if k == 6:
            w_gather.arrive(0)
            w_gather.arrive(1)

    for g in range(len(GROUPS)):
        first, count = x_slots(g)
        for n in range(1, NX):
            src = wrap(x + n, NX)
            part = r_x.at[src, pl.ds(first, count)]
            copy(part, part, x_send.at[n, g], x_recv.at[src, g], at_x(n)).wait_recv()

    def slots_of(p):
        a, b = PIECES[p]
        return pl.ds(2 * a, 2 * (b - a))

    def y_part(step, p):
        return raw.at[wrap(y + step, NY), slots_of(p)]

    for p, (a, b) in enumerate(PIECES):
        for j in range(2 * a, 2 * b):
            code = own_ref[x, (j % 2) * (SLOTS // 2) + j // 2]
            raw[y, j] = r_x[code & (NX - 1), (code >> 2) & (CAP * NZ - 1)]
        own = y_part(0, p)
        go(copy(own, own, y_send.at[0, p], y_recv.at[0, p], at_y(r)))
        go(copy(own, own, y_send.at[1, p], y_recv.at[1, p], at_y(-r)))

    w_gather.arrive(2)
    for n in range(NY):
        w_gather.from_sibling(n)

    def y_arrive(n, p):
        piece = y_part((-1, 1, 2)[n] * r, p)
        copy(piece, piece, y_send.at[0, p], y_recv.at[n, p], at_y(r)).wait_recv()
        if n == 0:
            go(copy(piece, piece, y_send.at[2, p], y_recv.at[2, p], at_y(r)))

    def rows_of(p):
        a, b = PIECES[p]
        return pl.ds(16 * a, 16 * (b - a)), 16 * (b - a)

    def encode(step, p):
        chip = wrap(y + step, NY)
        rows, count = rows_of(p)
        here = 2 * chip + c
        rawf = raw[chip, slots_of(p)].astype(F32).reshape(count, ENC)
        mean_square = jnp.sum(rawf * rawf, axis=-1, keepdims=True) * (1.0 / ENC)
        normed = (rawf * lax.rsqrt(mean_square + 1e-06)).astype(BF16)
        for t in range(TILES // 2):
            w2 = jnp.concatenate([wenc[2 * t], wenc[2 * t + 1]], axis=1)
            summed = jnp.dot(normed, w2, preferred_element_type=F32)
            width = min(256, ENC - 256 * t)
            summed = summed[:, :width]
            part = rawf[:, 256 * t : 256 * t + width]
            enc[here, rows, 256 * t : 256 * t + width] = (part + summed * jax.nn.sigmoid(summed)).astype(BF16)
        own = enc.at[here, rows]
        delta = wrap(step, NY)
        go(copy(own, own, e_send.at[delta, p], e_recv.at[delta, p], sibling))

    def project(step, p):
        chip = wrap(y + step, NY)
        rows, n = rows_of(p)
        theirs = enc.at[2 * chip + 1 - c, rows]
        delta = wrap(step, NY)
        copy(theirs, theirs, e_send.at[delta, p], e_recv.at[delta, p], sibling).wait_recv()
        pair = pl.ds(2 * chip, 2)
        lhs = enc[pair, rows, :].reshape(2 * n, ENC)
        for w, out in ((wk, kbuf), (wv, vbuf)):
            got = jnp.dot(lhs, w[...], preferred_element_type=F32).astype(BF16)
            out[pair, rows, :] = got.reshape(2, n, COLS)

    def attend(chunk):
        first = chunk + lax.div(chunk, 5)
        token = lax.broadcasted_iota(jnp.int32, (ROWS, 128), 0) + ROWS * chunk
        span_of = token >> 6
        for hd in range(COLS // HEAD_DIM):
            cols = slice(hd * HEAD_DIM, (hd + 1) * HEAD_DIM)

            def window(ref):
                spans = []
                for s in range(3):
                    rows = pl.ds(pl.multiple_of(16 * (first + s), 16), 16)
                    spans.append(ref[:, rows, cols].reshape(128, HEAD_DIM))
                return jnp.concatenate(spans, axis=0)

            scores = lax.dot_general(
                qbuf[chunk, :, cols], window(kbuf), (((1,), (1,)), ((), ())),
                preferred_element_type=F32,
            ) * HEAD_DIM ** (-0.5)
            parts = [
                jnp.where(span_of == first + s, scores[:, 128 * s : 128 * s + 128], -1e30) for s in range(3)
            ]
            highest = jnp.max(jnp.maximum(jnp.maximum(parts[0], parts[1]), parts[2]), axis=-1, keepdims=True)
            weights = [jnp.exp(p - highest) for p in parts]
            total = jnp.sum(weights[0] + weights[1] + weights[2], axis=-1, keepdims=True)
            probs = jnp.concatenate([(w / total).astype(BF16) for w in weights], axis=1)
            mixed = jnp.dot(probs, window(vbuf), preferred_element_type=F32)
            obuf[chunk, :, cols] = mixed.astype(BF16)

    def out_copy(chunk):
        dev = (x, z, lax.div(chunk, NC), lax.rem(chunk, NC))
        return copy(obuf.at[chunk], out_ref.at[:, own_cols], o_send.at[chunk], o_recv.at[h], dev)

    own_out = pltpu.make_async_copy(obuf.at[h], out_ref.at[:, own_cols], local.at[5])

    encode(0, 0)
    y_arrive(0, 0)
    encode(0, 1)
    y_arrive(0, 1)
    locals_[2].wait()
    locals_[3].wait()
    for p in range(2):
        encode(-r, p)
        y_arrive(1, p)
        encode(r, p)
        project(0, p)
        for step in (1, -1):
            project(step, p)
        y_arrive(2, p)
        encode(2, p)
        project(2, p)
        if p == 0:
            locals_[4].wait()
            for n, (dy, e) in enumerate(others):
                src = 2 * wrap(y + dy, NY) + wrap(c + e, NC)
                copy(qbuf.at[src], qbuf.at[src], q_send.at[n], q_recv.at[src], sibling).wait_recv()

        @pl.loop(p * CHUNKS // 2, (p + 1) * CHUNKS // 2)
        def _(chunk):
            attend(chunk)

            @pl.when(chunk == h)
            def _():
                own_out.start()

            @pl.when(chunk != h)
            def _():
                out_copy(chunk).start()

    own_out.wait()
    for dy, e in others:
        src = 2 * wrap(y + dy, NY) + wrap(c + e, NC)
        cols = pl.ds(pl.multiple_of(src * COLS, COLS), COLS)
        copy(obuf.at[h], out_ref.at[:, cols], o_send.at[src], o_recv.at[src], sibling).wait_recv()
    for cp in sends:
        cp.wait_send()
    for dy, e in others:
        out_copy(2 * wrap(y + dy, NY) + wrap(c + e, NC)).wait_send()


def cited(neighbour_ids):
    ids = neighbour_ids.T.reshape(CAP, NX, NZ, SLOTS // 2)
    ids = lax.dynamic_index_in_dim(ids, lax.axis_index("z"), 2, keepdims=False)
    rows = jnp.concatenate([ids[0], ids[1]], axis=1)
    return jnp.pad(rows, ((0, 8 - NX), (0, 128 - SLOTS)))


def per_device(queries, database_rows, w_encoder, w_key, w_value, neighbour_ids):
    padded = jnp.pad(w_encoder, ((0, 16 - WROWS), (0, 128 * TILES - ENC)))
    tiles = padded.reshape(16, TILES, 128).transpose(1, 0, 2)
    g, p = len(GROUPS), len(PIECES)
    dma = pltpu.SemaphoreType.DMA
    any_ = pl.BlockSpec(memory_space=pl.ANY)
    return pl.pallas_call(
        kernel,
        out_shape=jax.ShapeDtypeStruct(queries.shape, BF16),
        in_specs=[pl.BlockSpec(memory_space=pltpu.VMEM)] + [any_] * 5,
        out_specs=any_,
        scratch_shapes=[
            pltpu.VMEM((2, 8, 128), jnp.int32), pltpu.SMEM((8, 128), jnp.int32), pltpu.SMEM((8, 128), jnp.int32),
        ] + [pltpu.VMEM(((b - a) * ENTRIES, TOK, ENC), BF16) for a, b in GROUPS] + [
            pltpu.VMEM((NX, NZ, 16, 128), BF16),
            pltpu.VMEM((TILES, ENC, 128), BF16),
            pltpu.VMEM((ENC, COLS), BF16),
            pltpu.VMEM((ENC, COLS), BF16),
            pltpu.VMEM((CHUNKS, ROWS, COLS), BF16),
            pltpu.VMEM((NX - 1, CAP * NZ, TOK, ENC), BF16),
            pltpu.VMEM((NX, CAP * NZ, TOK, ENC), BF16),
            pltpu.VMEM((NY, SLOTS, TOK, ENC), BF16),
            pltpu.VMEM((CHUNKS, SLOTS * TOK, ENC), BF16),
            pltpu.VMEM((CHUNKS, SLOTS * TOK, COLS), BF16),
            pltpu.VMEM((CHUNKS, SLOTS * TOK, COLS), BF16),
            pltpu.VMEM((CHUNKS, ROWS, COLS), BF16),
            dma((2, NZ // 2, SUB)), dma((2, NZ // 2, SUB)),
            dma((NZ,)), dma((NZ,)),
            dma((8,)),
            dma((7,)), dma((CHUNKS,)),
            dma((NX,)), dma((NX,)),
            dma((7,)), dma((3,)), dma((NY,)),
            dma((NX, g)), dma((NX, g)),
            dma((3, p)), dma((3, p)),
            dma((NY, p)), dma((NY, p)),
            dma((CHUNKS,)), dma((CHUNKS,)),
        ],
        compiler_params=pltpu.CompilerParams(collective_id=0, has_side_effects=True),
        name="exchange_attend",
    )(cited(neighbour_ids), database_rows, tiles, queries, w_key, w_value)


def solution(mesh):
    torus = Mesh(mesh.devices.reshape(NX, NZ, NY, NC), SEQ_HEAD)
    in_specs = (
        P(SEQ_HEAD, None), P(SEQ, HEAD, None), P(SEQ, None), P(None, HEAD), P(None, HEAD), P(),
    )
    return jax.shard_map(
        per_device, mesh=torus, in_specs=in_specs, out_specs=P(SEQ_HEAD, None), check_vma=False
    )
```

time: 97.4 us -> 93.1 us (0.956)
  Pallas kernels: 91.4 us -> 88.6 us
  local copies, waits for them, and re-layouts: 5.77 us -> 4.13 us
    unnamed x10 -> x3, local copies, waits for them, and re-layouts: 4.8 us -> 2.02 us
    pallas_call x1, Pallas kernels: 91.4 us -> 88.6 us  [per_device(): pl.pallas_call(kernel, out_shape=jax.ShapeDtypeStruct(queries.shape, BF16...]
where the time goes in v2:
time: 93.1 us; the launch traced here: 92.8 us
  Pallas kernels  88.6 us (95%)
  local copies, waits for them, and re-layouts  4.13 us (4%)
    pallas_call x1, Pallas kernels, per_device(): pl.pallas_call(kernel, out_shape=jax.ShapeDtypeStruct(queries.shape, BF16...  88.6 us
    unnamed x3, local copies, waits for them, and re-layouts  2.02 us

profile of v2, /device:TPU:1, one launch (start us, length us, event | category | flops | bytes accessed | tf_op | source)
XLA Modules:
  0.0 92.8 jit_solution(8927846409677948246)
XLA Ops:
  0.0 0.0 copy-start
  0.0 1.4 %bitcast_bitcast_fusion.wsh_ref = bf16[8,16,128]{2,1,0:T(8,128)(2,1)} fusion(bf16[14,896]{1,0:T(8,128)(2,1)} %param.8), kind=kLoop, calls=%fused_computation | loop fusion | bytes 57856 | tf_op jit(solution)/shard_map/transpose | solution.py:420
  1.4 0.0 copy-done
  1.4 0.1 reshape.10
  1.6 0.1 pad_add_fusion
  1.6 0.6 pad.8.ids_ref
  2.2 88.6 %exchange_attend.1 = bf16[88,4096]{1,0:T(8,128)(2,1)} custom-call(s32[8,128]{1,0:T(8,128)} %pad.8.ids_ref, bf16[8,8,896]{2,1,0:T(8,128)(2,1)} %db_ref.1, bf16[8,16,128]{2,1,0:T(8,128)(2,1)} %bitcast_bitcast_fusion.wsh_ref, bf16[88,4096]{1,0:T(8,128)(2,1)} %q_ref.1, bf16[896,512]{1,0:T(8,128)(2,1)} %wk_ref.1, bf16[896,512]{1,0:T(8,128)(2,1)} %wv_ref.1), custom_call_target="tpu_custom_call" | custom-call | tf_op jit(solution)/shard_map/exchange_attend/pallas_call | solution.py:424
  90.8 2.0 %copy.12 = bf16[88,4096]{1,0:T(8,128)(2,1)} copy(bf16[88,4096]{1,0:T(8,128)(2,1)} %exchange_attend.1) | data formatting | bytes 1441792
  (1 shorter events, 0.0 us)
Async XLA Ops:
  0.0 1.4 %copy-start = (s32[704,2]{0,1:T(2,128)S(1)}, s32[704,2]{0,1:T(2,128)}, u32[]{:S(2)}) copy-start(s32[704,2]{0,1:T(2,128)} %param.11) | copy-start | bytes 16900

commit v3 on v2

--- a/solution.py
+++ b/solution.py
@@ -30,7 +30,11 @@
 
 GROUPS = ((0, 5), (5, 9), (9, 13), (13, 16))
 READY = {1: 0, 3: 1, 5: 2, 7: 3}
-PIECES = ((0, 6), (6, 11))
+
+SPAN = 64
+SPANS = (0, 1, 4, 5, 6, 9, 10, 2, 3, 7, 8)
+PIECES = ((0, 7), (7, 11))
+HALVES = ((0, 3, 4, 7), (1, 2, 5, 6))
 
 
 def order_of(d, way):
@@ -38,8 +42,8 @@
 
 
 def kernel(
-    ids_ref, db_ref, wsh_ref, q_ref, wk_ref, wv_ref, out_ref,
-    vtab, inv_ref, own_ref, z0, z1, z2, z3, wz, wenc, wk, wv, qbuf, s_x, r_x, raw, enc, kbuf, vbuf, obuf,
+    ids_hbm, db_ref, wsh_ref, q_ref, wk_ref, wv_ref, out_ref,
+    ids_ref, vtab, inv_ref, own_ref, z0, z1, z2, z3, wz, wenc, wk, wv, qbuf, s_x, r_x, raw, enc, kbuf, vbuf, mixed, obuf,
     z_send, z_recv, wz_send, wz_recv, local, q_send, q_recv,
     wx_send, wx_recv, wy_send, wy_recv, wy_sib, x_send, x_recv,
     y_send, y_recv, e_send, e_recv, o_send, o_recv,
@@ -73,6 +77,9 @@
 
     def at_head(dy, e):
         return (x, z, wrap(y + dy, NY), wrap(c + e, NC))
+
+    read_ids = pltpu.make_async_copy(ids_hbm, ids_ref, local.at[8])
+    read_ids.start()
 
     barrier = pltpu.get_barrier_semaphore()
     partners = [at_z(s * d) for d in range(1, LEAP + 1) for s in (1, -1)]
@@ -126,6 +133,7 @@
     for cp in locals_:
         cp.start()
 
+    read_ids.wait()
     ids = ids_ref[...]
     lane = lax.broadcasted_iota(jnp.int32, (8, 128), 1)
     owner_of = ids >> 3
@@ -279,7 +287,7 @@
 
     for p, (a, b) in enumerate(PIECES):
         for j in range(2 * a, 2 * b):
-            code = own_ref[x, (j % 2) * (SLOTS // 2) + j // 2]
+            code = own_ref[x, (j % 2) * (SLOTS // 2) + SPANS[j // 2]]
             raw[y, j] = r_x[code & (NX - 1), (code >> 2) & (CAP * NZ - 1)]
         own = y_part(0, p)
         go(copy(own, own, y_send.at[0, p], y_recv.at[0, p], at_y(r)))
@@ -329,36 +337,50 @@
             got = jnp.dot(lhs, w[...], preferred_element_type=F32).astype(BF16)
             out[pair, rows, :] = got.reshape(2, n, COLS)
 
-    def attend(chunk):
-        first = chunk + lax.div(chunk, 5)
-        token = lax.broadcasted_iota(jnp.int32, (ROWS, 128), 0) + ROWS * chunk
-        span_of = token >> 6
-        for hd in range(COLS // HEAD_DIM):
-            cols = slice(hd * HEAD_DIM, (hd + 1) * HEAD_DIM)
-
-            def window(ref):
-                spans = []
-                for s in range(3):
-                    rows = pl.ds(pl.multiple_of(16 * (first + s), 16), 16)
-                    spans.append(ref[:, rows, cols].reshape(128, HEAD_DIM))
-                return jnp.concatenate(spans, axis=0)
-
-            scores = lax.dot_general(
-                qbuf[chunk, :, cols], window(kbuf), (((1,), (1,)), ((), ())),
-                preferred_element_type=F32,
-            ) * HEAD_DIM ** (-0.5)
-            parts = [
-                jnp.where(span_of == first + s, scores[:, 128 * s : 128 * s + 128], -1e30) for s in range(3)
-            ]
-            highest = jnp.max(jnp.maximum(jnp.maximum(parts[0], parts[1]), parts[2]), axis=-1, keepdims=True)
-            weights = [jnp.exp(p - highest) for p in parts]
-            total = jnp.sum(weights[0] + weights[1] + weights[2], axis=-1, keepdims=True)
-            probs = jnp.concatenate([(w / total).astype(BF16) for w in weights], axis=1)
-            mixed = jnp.dot(probs, window(vbuf), preferred_element_type=F32)
-            obuf[chunk, :, cols] = mixed.astype(BF16)
+    def attend(spans):
+        heads = [slice(hd * HEAD_DIM, (hd + 1) * HEAD_DIM) for hd in range(COLS // HEAD_DIM)]
+        pairs = [(span, cols) for span in spans for cols in heads]
+        scores = []
+        for span, cols in pairs:
+            first, last = SPAN * span, SPAN * (span + 1)
+            rows = []
+            for chunk in range(first // ROWS, (last - 1) // ROWS + 1):
+                a, b = max(first - ROWS * chunk, 0), min(last - ROWS * chunk, ROWS)
+                rows.append(qbuf[chunk, :, cols].astype(F32)[a:b])
+            q = jnp.concatenate(rows, axis=0).astype(BF16)
+            at = 16 * SPANS.index(span)
+            k = kbuf[:, at : at + 16, cols].reshape(128, HEAD_DIM)
+            scores.append(lax.dot_general(q, k, (((1,), (1,)), ((), ())), preferred_element_type=F32))
+        scores = jnp.concatenate(scores, axis=0) * HEAD_DIM ** (-0.5)
+        weights = jnp.exp(scores - jnp.max(scores, axis=-1, keepdims=True))
+        scale = 1.0 / jnp.sum(weights, axis=-1, keepdims=True)
+        probs = (weights * scale).astype(BF16)
+        outs = []
+        for n, (span, cols) in enumerate(pairs):
+            at = 16 * SPANS.index(span)
+            v = vbuf[:, at : at + 16, cols].reshape(128, HEAD_DIM)
+            outs.append(jnp.dot(probs[SPAN * n : SPAN * (n + 1)], v, preferred_element_type=F32))
+        for out, (span, cols) in zip(outs, pairs):
+            mixed[span, :, cols] = out
+
+    def finish(chunk):
+        first, last = ROWS * chunk, ROWS * (chunk + 1)
+        rows = []
+        for span in range(first // SPAN, (last - 1) // SPAN + 1):
+            a, b = max(first - SPAN * span, 0), min(last - SPAN * span, SPAN)
+            rows.append(mixed[span, a:b, :])
+        obuf[chunk] = jnp.concatenate(rows, axis=0).astype(BF16)
+
+        @pl.when(h == chunk)
+        def _():
+            own_out.start()
+
+        @pl.when(h != chunk)
+        def _():
+            out_copy(chunk).start()
 
     def out_copy(chunk):
-        dev = (x, z, lax.div(chunk, NC), lax.rem(chunk, NC))
+        dev = (x, z, chunk // NC, chunk % NC)
         return copy(obuf.at[chunk], out_ref.at[:, own_cols], o_send.at[chunk], o_recv.at[h], dev)
 
     own_out = pltpu.make_async_copy(obuf.at[h], out_ref.at[:, own_cols], local.at[5])
@@ -373,29 +395,29 @@
         encode(-r, p)
         y_arrive(1, p)
         encode(r, p)
-        project(0, p)
-        for step in (1, -1):
-            project(step, p)
-        y_arrive(2, p)
-        encode(2, p)
-        project(2, p)
-        if p == 0:
-            locals_[4].wait()
-            for n, (dy, e) in enumerate(others):
-                src = 2 * wrap(y + dy, NY) + wrap(c + e, NC)
-                copy(qbuf.at[src], qbuf.at[src], q_send.at[n], q_recv.at[src], sibling).wait_recv()
-
-        @pl.loop(p * CHUNKS // 2, (p + 1) * CHUNKS // 2)
-        def _(chunk):
-            attend(chunk)
-
-            @pl.when(chunk == h)
-            def _():
-                own_out.start()
-
-            @pl.when(chunk != h)
-            def _():
-                out_copy(chunk).start()
+    for step, p in ((0, 0), (r, 0), (-r, 0), (0, 1)):
+        project(step, p)
+    locals_[4].wait()
+    for n, (dy, e) in enumerate(others):
+        src = 2 * wrap(y + dy, NY) + wrap(c + e, NC)
+        copy(qbuf.at[src], qbuf.at[src], q_send.at[n], q_recv.at[src], sibling).wait_recv()
+    y_arrive(2, 0)
+    encode(2, 0)
+    for step, p in ((r, 1), (-r, 1), (2, 0)):
+        project(step, p)
+    for chunks, spans in zip(HALVES[0], ((0, 1), (4, 5), (6,), (9, 10))):
+        attend(spans)
+        finish(chunks)
+        if chunks == HALVES[0][1]:
+            y_arrive(2, 1)
+            encode(2, 1)
+    project(2, 1)
+    attend((2, 3))
+    finish(1)
+    finish(2)
+    attend((7, 8))
+    finish(5)
+    finish(6)
 
     own_out.wait()
     for dy, e in others:
@@ -405,7 +427,7 @@
     for cp in sends:
         cp.wait_send()
     for dy, e in others:
-        out_copy(2 * wrap(y + dy, NY) + wrap(c + e, NC)).wait_send()
+        copy(obuf.at[h], obuf.at[h], o_send.at[2 * wrap(y + dy, NY) + wrap(c + e, NC)], o_recv.at[h], sibling).wait_send()
 
 
 def cited(neighbour_ids):
@@ -424,9 +446,10 @@
     return pl.pallas_call(
         kernel,
         out_shape=jax.ShapeDtypeStruct(queries.shape, BF16),
-        in_specs=[pl.BlockSpec(memory_space=pltpu.VMEM)] + [any_] * 5,
+        in_specs=[any_] * 6,
         out_specs=any_,
         scratch_shapes=[
+            pltpu.VMEM((8, 128), jnp.int32),
             pltpu.VMEM((2, 8, 128), jnp.int32), pltpu.SMEM((8, 128), jnp.int32), pltpu.SMEM((8, 128), jnp.int32),
         ] + [pltpu.VMEM(((b - a) * ENTRIES, TOK, ENC), BF16) for a, b in GROUPS] + [
             pltpu.VMEM((NX, NZ, 16, 128), BF16),
@@ -440,10 +463,11 @@
             pltpu.VMEM((CHUNKS, SLOTS * TOK, ENC), BF16),
             pltpu.VMEM((CHUNKS, SLOTS * TOK, COLS), BF16),
             pltpu.VMEM((CHUNKS, SLOTS * TOK, COLS), BF16),
+            pltpu.VMEM((SLOTS // 2, SPAN, COLS), F32),
             pltpu.VMEM((CHUNKS, ROWS, COLS), BF16),
             dma((2, NZ // 2, SUB)), dma((2, NZ // 2, SUB)),
             dma((NZ,)), dma((NZ,)),
-            dma((8,)),
+            dma((9,)),
             dma((7,)), dma((CHUNKS,)),
             dma((NX,)), dma((NX,)),
             dma((7,)), dma((3,)), dma((NY,)),

time: 93.1 us -> 81.1 us (0.87)
  Pallas kernels: 88.6 us -> 76.4 us
    pallas_call x1, Pallas kernels: 88.6 us -> 76.4 us  [per_device(): pl.pallas_call(kernel, out_shape=jax.ShapeDtypeStruct(queries.shape, BF16...]
where the time goes in v3:
time: 81.1 us; the launch traced here: 80.7 us
  Pallas kernels  76.4 us (94%)
  local copies, waits for them, and re-layouts  4.13 us (5%)
    pallas_call x1, Pallas kernels, per_device(): pl.pallas_call(kernel, out_shape=jax.ShapeDtypeStruct(queries.shape, BF16...  76.4 us
    unnamed x3, local copies, waits for them, and re-layouts  2.02 us

profile of v3, /device:TPU:1, one launch (start us, length us, event | category | flops | bytes accessed | tf_op | source)
XLA Modules:
  0.0 80.7 jit_solution(15250448904830297653)
XLA Ops:
  0.0 0.0 copy-start
  0.0 1.4 %bitcast_bitcast_fusion.wsh_ref = bf16[8,16,128]{2,1,0:T(8,128)(2,1)} fusion(bf16[14,896]{1,0:T(8,128)(2,1)} %param.8), kind=kLoop, calls=%fused_computation | loop fusion | bytes 57856 | tf_op jit(solution)/shard_map/transpose | solution.py:442
  1.4 0.0 copy-done
  1.4 0.1 reshape.10
  1.6 0.1 pad_add_fusion
  1.6 0.6 pad.8.ids_hbm
  2.2 76.4 %exchange_attend.1 = bf16[88,4096]{1,0:T(8,128)(2,1)} custom-call(s32[8,128]{1,0:T(8,128)} %pad.8.ids_hbm, bf16[8,8,896]{2,1,0:T(8,128)(2,1)} %db_ref.1, bf16[8,16,128]{2,1,0:T(8,128)(2,1)} %bitcast_bitcast_fusion.wsh_ref, bf16[88,4096]{1,0:T(8,128)(2,1)} %q_ref.1, bf16[896,512]{1,0:T(8,128)(2,1)} %wk_ref.1, bf16[896,512]{1,0:T(8,128)(2,1)} %wv_ref.1), custom_call_target="tpu_custom_call" | custom-call | tf_op jit(solution)/shard_map/exchange_attend/pallas_call | solution.py:446
  78.7 2.0 %copy.12 = bf16[88,4096]{1,0:T(8,128)(2,1)} copy(bf16[88,4096]{1,0:T(8,128)(2,1)} %exchange_attend.1) | data formatting | bytes 1441792
  (1 shorter events, 0.0 us)
Async XLA Ops:
  0.0 1.4 %copy-start = (s32[704,2]{0,1:T(2,128)S(1)}, s32[704,2]{0,1:T(2,128)}, u32[]{:S(2)}) copy-start(s32[704,2]{0,1:T(2,128)} %param.11) | copy-start | bytes 16900

commit v4 on v3

--- a/solution.py
+++ b/solution.py
@@ -28,8 +28,7 @@
 TILES = 8
 LEAP = 4
 
-GROUPS = ((0, 5), (5, 9), (9, 13), (13, 16))
-READY = {1: 0, 3: 1, 5: 2, 7: 3}
+GROUPS = ((0, 1),) + tuple((2 * d - 1, min(2 * d + 1, NZ)) for d in range(1, NZ // 2 + 1))
 
 SPAN = 64
 SPANS = (0, 1, 4, 5, 6, 9, 10, 2, 3, 7, 8)
@@ -43,7 +42,7 @@
 
 def kernel(
     ids_hbm, db_ref, wsh_ref, q_ref, wk_ref, wv_ref, out_ref,
-    ids_ref, vtab, inv_ref, own_ref, z0, z1, z2, z3, wz, wenc, wk, wv, qbuf, s_x, r_x, raw, enc, kbuf, vbuf, mixed, obuf,
+    few_ref, ids_ref, wsh, vtab, inv_ref, own_ref, z0, z1, z2, z3, z4, z5, z6, z7, z8, wz, wenc, wk, wv, qbuf, s_x, r_x, raw, enc, kbuf, vbuf, mixed, obuf,
     z_send, z_recv, wz_send, wz_recv, local, q_send, q_recv,
     wx_send, wx_recv, wy_send, wy_recv, wy_sib, x_send, x_recv,
     y_send, y_recv, e_send, e_recv, o_send, o_recv,
@@ -51,7 +50,7 @@
     x, z, y, c = (lax.axis_index(a) for a in SEQ_HEAD)
     r = 1 - 2 * c
     h = 2 * y + c
-    zg = (z0, z1, z2, z3)
+    zg = (z0, z1, z2, z3, z4, z5, z6, z7, z8)
 
     def wrap(v, n):
         return lax.rem(v + 2 * n, n)
@@ -78,7 +77,9 @@
     def at_head(dy, e):
         return (x, z, wrap(y + dy, NY), wrap(c + e, NC))
 
-    read_ids = pltpu.make_async_copy(ids_hbm, ids_ref, local.at[8])
+    read_ids = pltpu.make_async_copy(ids_hbm, few_ref, local.at[8])
+    read_w = pltpu.make_async_copy(wsh_ref, wsh, local.at[1])
+    read_w.start()
     read_ids.start()
 
     barrier = pltpu.get_barrier_semaphore()
@@ -86,6 +87,11 @@
     partners += [at_x(n) for n in range(1, NX)] + [at_head(*o) for o in others]
     for dev in partners:
         pl.semaphore_signal(barrier, inc=1, device_id=dev, device_id_type=MESH)
+
+    read_w.wait()
+    tile = pl.multiple_of((h - lax.div(h, TILES - 1)) * 128, 128)
+    wz[x, 0] = jnp.zeros((16, 128), BF16)
+    wz[x, 0, :WROWS, :] = wsh[:, pl.ds(tile, 128)]
     pl.semaphore_wait(barrier, len(partners))
 
     sends = []
@@ -99,7 +105,7 @@
 
     for n, d in enumerate([s * d for d in range(1, LEAP + 1) for s in (1, -1)]):
         slot = d % NZ
-        go(copy(wsh_ref.at[h], wz.at[x, slot], wz_send.at[n], wz_recv.at[slot], at_z(r * d)))
+        go(copy(wz.at[x, 0], wz.at[x, slot], wz_send.at[n], wz_recv.at[slot], at_z(r * d)))
 
     def zpiece(place, i):
         g = next(k for k, (a, b) in enumerate(GROUPS) if a <= place < b)
@@ -125,7 +131,6 @@
     own_cols = pl.ds(pl.multiple_of(h * COLS, COLS), COLS)
     locals_ = [
         pltpu.make_async_copy(db_ref, z0.at[pl.ds(0, ENTRIES)], local.at[0]),
-        pltpu.make_async_copy(wsh_ref.at[h], wz.at[x, 0], local.at[1]),
         pltpu.make_async_copy(wk_ref, wk, local.at[2]),
         pltpu.make_async_copy(wv_ref, wv, local.at[3]),
         pltpu.make_async_copy(q_ref.at[:, own_cols], qbuf.at[h], local.at[4]),
@@ -134,6 +139,8 @@
         cp.start()
 
     read_ids.wait()
+    ids_ref[...] = jnp.zeros((8, 128), jnp.int32)
+    ids_ref[:NX, :SLOTS] = few_ref[...]
     ids = ids_ref[...]
     lane = lax.broadcasted_iota(jnp.int32, (8, 128), 1)
     owner_of = ids >> 3
@@ -194,7 +201,6 @@
         for slot in range(1, NZ):
             if slot not in (LEAP, NZ - LEAP):
                 w_arrived(slot)
-        locals_[1].wait()
         for n in range(1, NX):
             go(copy(wz.at[x], wz.at[x], wx_send.at[n], wx_recv.at[x], at_x(n)))
 
@@ -257,12 +263,12 @@
     locals_[0].wait()
     for cp in to_scalar:
         cp.wait()
+    x_exchange(0)
     for k in range(NZ // 2):
         z_step(k)
         if k == 0:
             w_leap()
-        if k in READY:
-            x_exchange(READY[k])
+        x_exchange(k + 1)
         if k == 2:
             w_columns()
         if k == 4:
@@ -285,13 +291,17 @@
     def y_part(step, p):
         return raw.at[wrap(y + step, NY), slots_of(p)]
 
+    def y_start(p):
+        own = y_part(0, p)
+        go(copy(own, own, y_send.at[0, p], y_recv.at[0, p], at_y(r)))
+        go(copy(own, own, y_send.at[1, p], y_recv.at[1, p], at_y(-r)))
+
     for p, (a, b) in enumerate(PIECES):
         for j in range(2 * a, 2 * b):
             code = own_ref[x, (j % 2) * (SLOTS // 2) + SPANS[j // 2]]
             raw[y, j] = r_x[code & (NX - 1), (code >> 2) & (CAP * NZ - 1)]
-        own = y_part(0, p)
-        go(copy(own, own, y_send.at[0, p], y_recv.at[0, p], at_y(r)))
-        go(copy(own, own, y_send.at[1, p], y_recv.at[1, p], at_y(-r)))
+        if p == 0:
+            y_start(p)
 
     w_gather.arrive(2)
     for n in range(NY):
@@ -387,30 +397,40 @@
 
     encode(0, 0)
     y_arrive(0, 0)
+    y_start(1)
+    encode(-r, 0)
+    y_arrive(1, 0)
+    encode(r, 0)
+    locals_[1].wait()
+    locals_[2].wait()
+    project(0, 0)
     encode(0, 1)
-    y_arrive(0, 1)
-    locals_[2].wait()
+    project(r, 0)
+    project(-r, 0)
+    project(0, 1)
     locals_[3].wait()
-    for p in range(2):
-        encode(-r, p)
-        y_arrive(1, p)
-        encode(r, p)
-    for step, p in ((0, 0), (r, 0), (-r, 0), (0, 1)):
-        project(step, p)
-    locals_[4].wait()
     for n, (dy, e) in enumerate(others):
         src = 2 * wrap(y + dy, NY) + wrap(c + e, NC)
         copy(qbuf.at[src], qbuf.at[src], q_send.at[n], q_recv.at[src], sibling).wait_recv()
     y_arrive(2, 0)
     encode(2, 0)
-    for step, p in ((r, 1), (-r, 1), (2, 0)):
-        project(step, p)
-    for chunks, spans in zip(HALVES[0], ((0, 1), (4, 5), (6,), (9, 10))):
-        attend(spans)
-        finish(chunks)
-        if chunks == HALVES[0][1]:
-            y_arrive(2, 1)
-            encode(2, 1)
+    y_arrive(0, 1)
+    encode(-r, 1)
+    project(2, 0)
+    attend((0, 1))
+    finish(0)
+    y_arrive(1, 1)
+    encode(r, 1)
+    attend((4, 5))
+    finish(3)
+    project(r, 1)
+    attend((6,))
+    finish(4)
+    project(-r, 1)
+    attend((9, 10))
+    finish(7)
+    y_arrive(2, 1)
+    encode(2, 1)
     project(2, 1)
     attend((2, 3))
     finish(1)
@@ -433,13 +453,10 @@
 def cited(neighbour_ids):
     ids = neighbour_ids.T.reshape(CAP, NX, NZ, SLOTS // 2)
     ids = lax.dynamic_index_in_dim(ids, lax.axis_index("z"), 2, keepdims=False)
-    rows = jnp.concatenate([ids[0], ids[1]], axis=1)
-    return jnp.pad(rows, ((0, 8 - NX), (0, 128 - SLOTS)))
+    return jnp.concatenate([ids[0], ids[1]], axis=1)
 
 
 def per_device(queries, database_rows, w_encoder, w_key, w_value, neighbour_ids):
-    padded = jnp.pad(w_encoder, ((0, 16 - WROWS), (0, 128 * TILES - ENC)))
-    tiles = padded.reshape(16, TILES, 128).transpose(1, 0, 2)
     g, p = len(GROUPS), len(PIECES)
     dma = pltpu.SemaphoreType.DMA
     any_ = pl.BlockSpec(memory_space=pl.ANY)
@@ -449,7 +466,9 @@
         in_specs=[any_] * 6,
         out_specs=any_,
         scratch_shapes=[
+            pltpu.VMEM((NX, SLOTS), jnp.int32),
             pltpu.VMEM((8, 128), jnp.int32),
+            pltpu.VMEM((WROWS, ENC), BF16),
             pltpu.VMEM((2, 8, 128), jnp.int32), pltpu.SMEM((8, 128), jnp.int32), pltpu.SMEM((8, 128), jnp.int32),
         ] + [pltpu.VMEM(((b - a) * ENTRIES, TOK, ENC), BF16) for a, b in GROUPS] + [
             pltpu.VMEM((NX, NZ, 16, 128), BF16),
@@ -478,7 +497,7 @@
         ],
         compiler_params=pltpu.CompilerParams(collective_id=0, has_side_effects=True),
         name="exchange_attend",
-    )(cited(neighbour_ids), database_rows, tiles, queries, w_key, w_value)
+    )(cited(neighbour_ids), database_rows, w_encoder, queries, w_key, w_value)
 
 
 def solution(mesh):

time: 81.1 us -> 79.6 us (0.982)
  local copies, waits for them, and re-layouts: 4.13 us -> 2.86 us
  Pallas kernels: 76.4 us -> 75.4 us
    transpose x1 -> x0, local copies, waits for them, and re-layouts: 1.38 us -> none  [per_device(): tiles = padded.reshape(16, TILES, 128).transpose(1, 0, 2)]
    pallas_call x1, Pallas kernels: 76.4 us -> 75.4 us  [per_device(): pl.pallas_call(kernel, out_shape=jax.ShapeDtypeStruct(queries.shape, BF16...]
where the time goes in v4:
time: 79.6 us; the launch traced here: 78.9 us
  Pallas kernels  75.4 us (95%)
  local copies, waits for them, and re-layouts  2.86 us (4%)
    pallas_call x1, Pallas kernels, per_device(): pl.pallas_call(kernel, out_shape=jax.ShapeDtypeStruct(queries.shape, BF16...  75.4 us
    unnamed x3, local copies, waits for them, and re-layouts  2.71 us

profile of v4, /device:TPU:1, one launch (start us, length us, event | category | flops | bytes accessed | tf_op | source)
XLA Modules:
  0.0 78.9 jit_solution(4399242194521550140)
XLA Ops:
  0.0 0.0 copy-start
  0.0 0.7 copy-done
  0.7 0.1 reshape.7
  0.9 0.7 pad_add_fusion.ids_hbm
  1.5 75.4 %exchange_attend.1 = bf16[88,4096]{1,0:T(8,128)(2,1)} custom-call(s32[4,22]{1,0:T(4,128)} %pad_add_fusion.ids_hbm, bf16[8,8,896]{2,1,0:T(8,128)(2,1)} %db_ref.1, bf16[14,896]{1,0:T(8,128)(2,1)} %wsh_ref.1, bf16[88,4096]{1,0:T(8,128)(2,1)} %q_ref.1, bf16[896,512]{1,0:T(8,128)(2,1)} %wk_ref.1, bf16[896,512]{1,0:T(8,128)(2,1)} %wv_ref.1), custom_call_target="tpu_custom_call" | custom-call | tf_op jit(solution)/shard_map/exchange_attend/pallas_call | solution.py:463
  76.9 2.0 %copy.9 = bf16[88,4096]{1,0:T(8,128)(2,1)} copy(bf16[88,4096]{1,0:T(8,128)(2,1)} %exchange_attend.1) | data formatting | bytes 1441792
  (1 shorter events, 0.0 us)
Async XLA Ops:
  0.0 0.7 copy-start

commit v5 on v4

--- a/solution.py
+++ b/solution.py
@@ -94,18 +94,18 @@
     wz[x, 0, :WROWS, :] = wsh[:, pl.ds(tile, 128)]
     pl.semaphore_wait(barrier, len(partners))
 
-    sends = []
-
-    def go(cp):
-        cp.start()
-        sends.append(cp)
-
-    def w_copy(n, slot, dist):
-        return copy(wz.at[x, slot], wz.at[x, slot], wz_send.at[n], wz_recv.at[slot], at_z(r * dist))
-
-    for n, d in enumerate([s * d for d in range(1, LEAP + 1) for s in (1, -1)]):
+    def sent(ref, sem):
+        copy(ref, ref, sem, q_recv.at[0], sibling).wait_send()
+
+    def arrived(ref, sem):
+        copy(ref, ref, q_send.at[0], sem, sibling).wait_recv()
+
+    def lane_of(slot):
+        return {LEAP: 0, NZ - LEAP: 1}.get(slot, 2)
+
+    for d in [s * d for d in range(1, LEAP + 1) for s in (1, -1)]:
         slot = d % NZ
-        go(copy(wz.at[x, 0], wz.at[x, slot], wz_send.at[n], wz_recv.at[slot], at_z(r * d)))
+        copy(wz.at[x, 0], wz.at[x, slot], wz_send.at[0], wz_recv.at[lane_of(slot)], at_z(r * d)).start()
 
     def zpiece(place, i):
         g = next(k for k, (a, b) in enumerate(GROUPS) if a <= place < b)
@@ -117,16 +117,16 @@
 
     for i in range(SUB):
         for way in range(2):
-            go(copy(
+            copy(
                 db_ref.at[pl.ds(i * (ENTRIES // SUB), ENTRIES // SUB)], zpiece(order_of(1, way), i),
-                z_send.at[way, 0, i], z_recv.at[way, 0, i], z_dev(way),
-            ))
-
-    for n, (dy, e) in enumerate(others):
+                z_send.at[way], z_recv.at[way, 0, i], z_dev(way),
+            ).start()
+
+    for dy, e in others:
         dev = at_head(dy, e)
         to = 2 * dev[2] + dev[3]
         cols = pl.ds(pl.multiple_of(to * COLS, COLS), COLS)
-        go(copy(q_ref.at[:, cols], qbuf.at[h], q_send.at[n], q_recv.at[h], dev))
+        copy(q_ref.at[:, cols], qbuf.at[h], q_send.at[0], q_recv.at[0], dev).start()
 
     own_cols = pl.ds(pl.multiple_of(h * COLS, COLS), COLS)
     locals_ = [
@@ -174,61 +174,48 @@
                 if d == NZ // 2 and way == 1:
                     continue
                 piece = zpiece(order_of(d, way), i)
-                copy(piece, piece, z_send.at[way, k, i], z_recv.at[way, k, i], z_dev(way)).wait_recv()
+                copy(piece, piece, z_send.at[way], z_recv.at[way, k, i], z_dev(way)).wait_recv()
                 if d + 1 < NZ // 2 or (d + 1 == NZ // 2 and way == 0):
-                    go(copy(
+                    copy(
                         piece, zpiece(order_of(d + 1, way), i),
-                        z_send.at[way, k + 1, i], z_recv.at[way, k + 1, i], z_dev(way),
-                    ))
-
-    def w_arrived(slot):
-        copy(wz.at[x, slot], wz.at[x, slot], wz_send.at[0], wz_recv.at[slot], at_z(1)).wait_recv()
+                        z_send.at[way], z_recv.at[way, k + 1, i], z_dev(way),
+                    ).start()
 
     def w_leap():
-        n = 2 * LEAP
         for s in (1, -1):
             held = s * LEAP % NZ
-            w_arrived(held)
+            arrived(wz.at[x, held], wz_recv.at[lane_of(held)])
             for d in range(1, LEAP + 1):
                 total = LEAP + d
                 if total == NZ // 2 and s == -1:
                     continue
                 slot = s * total % NZ
-                go(copy(wz.at[x, held], wz.at[x, slot], wz_send.at[n], wz_recv.at[slot], at_z(s * r * d)))
-                n += 1
+                copy(wz.at[x, held], wz.at[x, slot], wz_send.at[0], wz_recv.at[lane_of(slot)], at_z(s * r * d)).start()
 
     def w_columns():
-        for slot in range(1, NZ):
-            if slot not in (LEAP, NZ - LEAP):
-                w_arrived(slot)
+        arrived(wz.at[x, pl.ds(0, NZ - 3)], wz_recv.at[2])
         for n in range(1, NX):
-            go(copy(wz.at[x], wz.at[x], wx_send.at[n], wx_recv.at[x], at_x(n)))
+            copy(wz.at[x], wz.at[x], wx_send.at[0], wx_recv.at[0], at_x(n)).start()
 
     class Gather:
         def start(self):
             own = wenc.at[h]
-            go(copy(own, own, wy_send.at[0], wy_recv.at[0], at_y(r)))
-            go(copy(own, own, wy_send.at[1], wy_recv.at[1], at_y(-r)))
-            go(copy(own, own, wy_send.at[2], wy_sib.at[0], sibling))
+            copy(own, own, wy_send.at[0], wy_recv.at[0], at_y(r)).start()
+            copy(own, own, wy_send.at[0], wy_recv.at[1], at_y(-r)).start()
+            copy(own, own, wy_send.at[0], wy_sib.at[0], sibling).start()
 
         def arrive(self, n):
             step = (-1, 1, 2)[n] * r
             piece = wenc.at[2 * wrap(y + step, NY) + c]
             copy(piece, piece, wy_send.at[0], wy_recv.at[n], at_y(r)).wait_recv()
             if n == 0:
-                go(copy(piece, piece, wy_send.at[3], wy_recv.at[2], at_y(r)))
-            go(copy(piece, piece, wy_send.at[4 + n], wy_sib.at[wrap(step, NY)], sibling))
-
-        def from_sibling(self, delta):
-            piece = wenc.at[2 * wrap(y + delta, NY) + 1 - c]
-            copy(piece, piece, wy_send.at[0], wy_sib.at[delta], sibling).wait_recv()
+                copy(piece, piece, wy_send.at[0], wy_recv.at[2], at_y(r)).start()
+            copy(piece, piece, wy_send.at[0], wy_sib.at[0], sibling).start()
 
     w_gather = Gather()
 
     def w_pack():
-        for n in range(1, NX):
-            src = wrap(x + n, NX)
-            copy(wz.at[src], wz.at[src], wx_send.at[n], wx_recv.at[src], at_x(n)).wait_recv()
+        arrived(wz.at[pl.ds(0, NX - 1)], wx_recv.at[0])
         lhs_rows, rhs_rows = ENTRIES * WROWS, NZ * 16
         row = lax.broadcasted_iota(jnp.int32, (lhs_rows, rhs_rows), 0)
         col = lax.broadcasted_iota(jnp.int32, (lhs_rows, rhs_rows), 1)
@@ -258,7 +245,7 @@
                     r_x[x, j] = zg[g][at]
             if n:
                 part = pl.ds(first, count)
-                go(copy(s_x.at[n - 1, part], r_x.at[x, part], x_send.at[n, g], x_recv.at[x, g], at_x(n)))
+                copy(s_x.at[n - 1, part], r_x.at[x, part], x_send.at[0], x_recv.at[0], at_x(n)).start()
 
     locals_[0].wait()
     for cp in to_scalar:
@@ -277,12 +264,7 @@
             w_gather.arrive(0)
             w_gather.arrive(1)
 
-    for g in range(len(GROUPS)):
-        first, count = x_slots(g)
-        for n in range(1, NX):
-            src = wrap(x + n, NX)
-            part = r_x.at[src, pl.ds(first, count)]
-            copy(part, part, x_send.at[n, g], x_recv.at[src, g], at_x(n)).wait_recv()
+    arrived(s_x, x_recv.at[0])
 
     def slots_of(p):
         a, b = PIECES[p]
@@ -293,8 +275,8 @@
 
     def y_start(p):
         own = y_part(0, p)
-        go(copy(own, own, y_send.at[0, p], y_recv.at[0, p], at_y(r)))
-        go(copy(own, own, y_send.at[1, p], y_recv.at[1, p], at_y(-r)))
+        copy(own, own, y_send.at[0], y_recv.at[0, p], at_y(r)).start()
+        copy(own, own, y_send.at[0], y_recv.at[1, p], at_y(-r)).start()
 
     for p, (a, b) in enumerate(PIECES):
         for j in range(2 * a, 2 * b):
@@ -304,14 +286,13 @@
             y_start(p)
 
     w_gather.arrive(2)
-    for n in range(NY):
-        w_gather.from_sibling(n)
+    arrived(wenc.at[pl.ds(0, NY)], wy_sib.at[0])
 
     def y_arrive(n, p):
         piece = y_part((-1, 1, 2)[n] * r, p)
-        copy(piece, piece, y_send.at[0, p], y_recv.at[n, p], at_y(r)).wait_recv()
+        copy(piece, piece, y_send.at[0], y_recv.at[n, p], at_y(r)).wait_recv()
         if n == 0:
-            go(copy(piece, piece, y_send.at[2, p], y_recv.at[2, p], at_y(r)))
+            copy(piece, piece, y_send.at[0], y_recv.at[2, p], at_y(r)).start()
 
     def rows_of(p):
         a, b = PIECES[p]
@@ -333,14 +314,14 @@
             enc[here, rows, 256 * t : 256 * t + width] = (part + summed * jax.nn.sigmoid(summed)).astype(BF16)
         own = enc.at[here, rows]
         delta = wrap(step, NY)
-        go(copy(own, own, e_send.at[delta, p], e_recv.at[delta, p], sibling))
+        copy(own, own, e_send.at[0], e_recv.at[delta, p], sibling).start()
 
     def project(step, p):
         chip = wrap(y + step, NY)
         rows, n = rows_of(p)
         theirs = enc.at[2 * chip + 1 - c, rows]
         delta = wrap(step, NY)
-        copy(theirs, theirs, e_send.at[delta, p], e_recv.at[delta, p], sibling).wait_recv()
+        copy(theirs, theirs, e_send.at[0], e_recv.at[delta, p], sibling).wait_recv()
         pair = pl.ds(2 * chip, 2)
         lhs = enc[pair, rows, :].reshape(2 * n, ENC)
         for w, out in ((wk, kbuf), (wv, vbuf)):
@@ -391,7 +372,7 @@
 
     def out_copy(chunk):
         dev = (x, z, chunk // NC, chunk % NC)
-        return copy(obuf.at[chunk], out_ref.at[:, own_cols], o_send.at[chunk], o_recv.at[h], dev)
+        return copy(obuf.at[chunk], out_ref.at[:, own_cols], o_send.at[0], o_recv.at[0], dev)
 
     own_out = pltpu.make_async_copy(obuf.at[h], out_ref.at[:, own_cols], local.at[5])
 
@@ -409,9 +390,7 @@
     project(-r, 0)
     project(0, 1)
     locals_[3].wait()
-    for n, (dy, e) in enumerate(others):
-        src = 2 * wrap(y + dy, NY) + wrap(c + e, NC)
-        copy(qbuf.at[src], qbuf.at[src], q_send.at[n], q_recv.at[src], sibling).wait_recv()
+    arrived(qbuf.at[pl.ds(0, CHUNKS - 1)], q_recv.at[0])
     y_arrive(2, 0)
     encode(2, 0)
     y_arrive(0, 1)
@@ -440,14 +419,18 @@
     finish(6)
 
     own_out.wait()
-    for dy, e in others:
-        src = 2 * wrap(y + dy, NY) + wrap(c + e, NC)
-        cols = pl.ds(pl.multiple_of(src * COLS, COLS), COLS)
-        copy(obuf.at[h], out_ref.at[:, cols], o_send.at[src], o_recv.at[src], sibling).wait_recv()
-    for cp in sends:
-        cp.wait_send()
-    for dy, e in others:
-        copy(obuf.at[h], obuf.at[h], o_send.at[2 * wrap(y + dy, NY) + wrap(c + e, NC)], o_recv.at[h], sibling).wait_send()
+    some = pl.ds(0, CHUNKS - 1)
+    arrived(obuf.at[some], o_recv.at[0])
+    sent(obuf.at[some], o_send.at[0])
+    sent(qbuf.at[some], q_send.at[0])
+    sent(r_x.at[pl.ds(0, 2)], z_send.at[0])
+    sent(r_x.at[:, pl.ds(0, 14)], z_send.at[1])
+    sent(wz.at[0, pl.ds(0, NZ - 1)], wz_send.at[0])
+    sent(wz.at[pl.ds(0, NX - 1)], wx_send.at[0])
+    sent(wenc.at[pl.ds(0, TILES - 1)], wy_send.at[0])
+    sent(s_x, x_send.at[0])
+    sent(raw.at[pl.ds(0, NY - 1)], y_send.at[0])
+    sent(enc.at[pl.ds(0, NY)], e_send.at[0])
 
 
 def cited(neighbour_ids):
@@ -457,7 +440,7 @@
 
 
 def per_device(queries, database_rows, w_encoder, w_key, w_value, neighbour_ids):
-    g, p = len(GROUPS), len(PIECES)
+    p = len(PIECES)
     dma = pltpu.SemaphoreType.DMA
     any_ = pl.BlockSpec(memory_space=pl.ANY)
     return pl.pallas_call(
@@ -484,16 +467,16 @@
             pltpu.VMEM((CHUNKS, SLOTS * TOK, COLS), BF16),
             pltpu.VMEM((SLOTS // 2, SPAN, COLS), F32),
             pltpu.VMEM((CHUNKS, ROWS, COLS), BF16),
-            dma((2, NZ // 2, SUB)), dma((2, NZ // 2, SUB)),
-            dma((NZ,)), dma((NZ,)),
+            dma((2,)), dma((2, NZ // 2, SUB)),
+            dma((1,)), dma((3,)),
             dma((9,)),
-            dma((7,)), dma((CHUNKS,)),
-            dma((NX,)), dma((NX,)),
-            dma((7,)), dma((3,)), dma((NY,)),
-            dma((NX, g)), dma((NX, g)),
-            dma((3, p)), dma((3, p)),
-            dma((NY, p)), dma((NY, p)),
-            dma((CHUNKS,)), dma((CHUNKS,)),
+            dma((1,)), dma((1,)),
+            dma((1,)), dma((1,)),
+            dma((1,)), dma((3,)), dma((1,)),
+            dma((1,)), dma((1,)),
+            dma((1,)), dma((3, p)),
+            dma((1,)), dma((NY, p)),
+            dma((1,)), dma((1,)),
         ],
         compiler_params=pltpu.CompilerParams(collective_id=0, has_side_effects=True),
         name="exchange_attend",

time: 79.6 us -> 77.4 us (0.972)
  Pallas kernels: 75.4 us -> 73.3 us
    pallas_call x1, Pallas kernels: 75.4 us -> 73.3 us  [per_device(): pl.pallas_call(kernel, out_shape=jax.ShapeDtypeStruct(queries.shape, BF16...]
where the time goes in v5:
time: 77.4 us; the launch traced here: 76.8 us
  Pallas kernels  73.3 us (95%)
  local copies, waits for them, and re-layouts  2.86 us (4%)
    pallas_call x1, Pallas kernels, per_device(): pl.pallas_call(kernel, out_shape=jax.ShapeDtypeStruct(queries.shape, BF16...  73.3 us
    unnamed x3, local copies, waits for them, and re-layouts  2.71 us

profile of v5, /device:TPU:1, one launch (start us, length us, event | category | flops | bytes accessed | tf_op | source)
XLA Modules:
  0.0 76.8 jit_solution(15754080947445110551)
XLA Ops:
  0.0 0.0 copy-start
  0.0 0.7 copy-done
  0.7 0.1 reshape.7
  0.9 0.7 pad_add_fusion.ids_hbm
  1.5 73.3 %exchange_attend.1 = bf16[88,4096]{1,0:T(8,128)(2,1)} custom-call(s32[4,22]{1,0:T(4,128)} %pad_add_fusion.ids_hbm, bf16[8,8,896]{2,1,0:T(8,128)(2,1)} %db_ref.1, bf16[14,896]{1,0:T(8,128)(2,1)} %wsh_ref.1, bf16[88,4096]{1,0:T(8,128)(2,1)} %q_ref.1, bf16[896,512]{1,0:T(8,128)(2,1)} %wk_ref.1, bf16[896,512]{1,0:T(8,128)(2,1)} %wv_ref.1), custom_call_target="tpu_custom_call" | custom-call | tf_op jit(solution)/shard_map/exchange_attend/pallas_call | solution.py:446
  74.8 2.0 %copy.9 = bf16[88,4096]{1,0:T(8,128)(2,1)} copy(bf16[88,4096]{1,0:T(8,128)(2,1)} %exchange_attend.1) | data formatting | bytes 1441792
  (1 shorter events, 0.0 us)
Async XLA Ops:
  0.0 0.7 copy-start

commit v6 on v5

--- a/solution.py
+++ b/solution.py
@@ -26,7 +26,8 @@
 ROWS = 88
 CHUNKS = 8
 TILES = 8
-LEAP = 4
+LEAP = 2
+LEAPS = (NZ // 2 - 1) // LEAP
 
 GROUPS = ((0, 1),) + tuple((2 * d - 1, min(2 * d + 1, NZ)) for d in range(1, NZ // 2 + 1))
 
@@ -101,7 +102,10 @@
         copy(ref, ref, q_send.at[0], sem, sibling).wait_recv()
 
     def lane_of(slot):
-        return {LEAP: 0, NZ - LEAP: 1}.get(slot, 2)
+        for n in range(LEAPS):
+            if slot in (LEAP * (n + 1), NZ - LEAP * (n + 1)):
+                return 2 * n + (slot > NZ // 2)
+        return 2 * LEAPS
 
     for d in [s * d for d in range(1, LEAP + 1) for s in (1, -1)]:
         slot = d % NZ
@@ -181,19 +185,19 @@
                         z_send.at[way], z_recv.at[way, k + 1, i], z_dev(way),
                     ).start()
 
-    def w_leap():
+    def w_leap(number):
         for s in (1, -1):
-            held = s * LEAP % NZ
+            held = s * LEAP * number % NZ
             arrived(wz.at[x, held], wz_recv.at[lane_of(held)])
             for d in range(1, LEAP + 1):
-                total = LEAP + d
-                if total == NZ // 2 and s == -1:
+                total = LEAP * number + d
+                if total > NZ // 2 or (total == NZ // 2 and s == -1):
                     continue
                 slot = s * total % NZ
                 copy(wz.at[x, held], wz.at[x, slot], wz_send.at[0], wz_recv.at[lane_of(slot)], at_z(s * r * d)).start()
 
     def w_columns():
-        arrived(wz.at[x, pl.ds(0, NZ - 3)], wz_recv.at[2])
+        arrived(wz.at[x, pl.ds(0, NZ - 1 - 2 * LEAPS)], wz_recv.at[2 * LEAPS])
         for n in range(1, NX):
             copy(wz.at[x], wz.at[x], wx_send.at[0], wx_recv.at[0], at_x(n)).start()
 
@@ -253,14 +257,14 @@
     x_exchange(0)
     for k in range(NZ // 2):
         z_step(k)
-        if k == 0:
-            w_leap()
+        if k < LEAPS:
+            w_leap(k + 1)
         x_exchange(k + 1)
-        if k == 2:
+        if k == 3:
             w_columns()
-        if k == 4:
+        if k == 5:
             w_pack()
-        if k == 6:
+        if k == 7:
             w_gather.arrive(0)
             w_gather.arrive(1)
 
@@ -298,11 +302,12 @@
         a, b = PIECES[p]
         return pl.ds(16 * a, 16 * (b - a)), 16 * (b - a)
 
-    def encode(step, p):
-        chip = wrap(y + step, NY)
+    def encode(steps, p):
         rows, count = rows_of(p)
-        here = 2 * chip + c
-        rawf = raw[chip, slots_of(p)].astype(F32).reshape(count, ENC)
+        chips = [wrap(y + step, NY) for step in steps]
+        rawf = jnp.concatenate(
+            [raw[chip, slots_of(p)].astype(F32).reshape(count, ENC) for chip in chips], axis=0
+        )
         mean_square = jnp.sum(rawf * rawf, axis=-1, keepdims=True) * (1.0 / ENC)
         normed = (rawf * lax.rsqrt(mean_square + 1e-06)).astype(BF16)
         for t in range(TILES // 2):
@@ -311,22 +316,26 @@
             width = min(256, ENC - 256 * t)
             summed = summed[:, :width]
             part = rawf[:, 256 * t : 256 * t + width]
-            enc[here, rows, 256 * t : 256 * t + width] = (part + summed * jax.nn.sigmoid(summed)).astype(BF16)
-        own = enc.at[here, rows]
-        delta = wrap(step, NY)
-        copy(own, own, e_send.at[0], e_recv.at[delta, p], sibling).start()
-
-    def project(step, p):
-        chip = wrap(y + step, NY)
+            coded = (part + summed * jax.nn.sigmoid(summed)).astype(BF16)
+            for n, chip in enumerate(chips):
+                enc[2 * chip + c, rows, 256 * t : 256 * t + width] = coded[n * count : (n + 1) * count]
+        for step, chip in zip(steps, chips):
+            own = enc.at[2 * chip + c, rows]
+            copy(own, own, e_send.at[0], e_recv.at[wrap(step, NY), p], sibling).start()
+
+    def project(steps, p):
         rows, n = rows_of(p)
-        theirs = enc.at[2 * chip + 1 - c, rows]
-        delta = wrap(step, NY)
-        copy(theirs, theirs, e_send.at[0], e_recv.at[delta, p], sibling).wait_recv()
-        pair = pl.ds(2 * chip, 2)
-        lhs = enc[pair, rows, :].reshape(2 * n, ENC)
+        pairs = []
+        for step in steps:
+            chip = wrap(y + step, NY)
+            theirs = enc.at[2 * chip + 1 - c, rows]
+            copy(theirs, theirs, e_send.at[0], e_recv.at[wrap(step, NY), p], sibling).wait_recv()
+            pairs.append(pl.ds(2 * chip, 2))
+        lhs = jnp.concatenate([enc[pair, rows, :].reshape(2 * n, ENC) for pair in pairs], axis=0)
         for w, out in ((wk, kbuf), (wv, vbuf)):
             got = jnp.dot(lhs, w[...], preferred_element_type=F32).astype(BF16)
-            out[pair, rows, :] = got.reshape(2, n, COLS)
+            for m, pair in enumerate(pairs):
+                out[pair, rows, :] = got[2 * n * m : 2 * n * (m + 1)].reshape(2, n, COLS)
 
     def attend(spans):
         heads = [slice(hd * HEAD_DIM, (hd + 1) * HEAD_DIM) for hd in range(COLS // HEAD_DIM)]
@@ -376,41 +385,37 @@
 
     own_out = pltpu.make_async_copy(obuf.at[h], out_ref.at[:, own_cols], local.at[5])
 
-    encode(0, 0)
+    encode((0,), 0)
+    encode((0,), 1)
+    locals_[1].wait()
+    locals_[2].wait()
     y_arrive(0, 0)
     y_start(1)
-    encode(-r, 0)
     y_arrive(1, 0)
-    encode(r, 0)
-    locals_[1].wait()
-    locals_[2].wait()
-    project(0, 0)
-    encode(0, 1)
-    project(r, 0)
-    project(-r, 0)
-    project(0, 1)
+    encode((-r, r), 0)
+    project((0,), 0)
+    project((0,), 1)
+    project((-r, r), 0)
     locals_[3].wait()
     arrived(qbuf.at[pl.ds(0, CHUNKS - 1)], q_recv.at[0])
     y_arrive(2, 0)
-    encode(2, 0)
+    encode((2,), 0)
     y_arrive(0, 1)
-    encode(-r, 1)
-    project(2, 0)
+    y_arrive(1, 1)
+    encode((-r, r), 1)
+    project((2,), 0)
     attend((0, 1))
     finish(0)
-    y_arrive(1, 1)
-    encode(r, 1)
     attend((4, 5))
     finish(3)
-    project(r, 1)
+    project((-r, r), 1)
     attend((6,))
     finish(4)
-    project(-r, 1)
+    y_arrive(2, 1)
+    encode((2,), 1)
     attend((9, 10))
     finish(7)
-    y_arrive(2, 1)
-    encode(2, 1)
-    project(2, 1)
+    project((2,), 1)
     attend((2, 3))
     finish(1)
     finish(2)
@@ -468,7 +473,7 @@
             pltpu.VMEM((SLOTS // 2, SPAN, COLS), F32),
             pltpu.VMEM((CHUNKS, ROWS, COLS), BF16),
             dma((2,)), dma((2, NZ // 2, SUB)),
-            dma((1,)), dma((3,)),
+            dma((1,)), dma((2 * LEAPS + 1,)),
             dma((9,)),
             dma((1,)), dma((1,)),
             dma((1,)), dma((1,)),

time: 77.4 us -> 76.4 us (0.987)
  no operation moved by 1% of the time
where the time goes in v6:
time: 76.4 us; the launch traced here: 76.1 us
  Pallas kernels  72.6 us (95%)
  local copies, waits for them, and re-layouts  2.86 us (4%)
    pallas_call x1, Pallas kernels, per_device(): pl.pallas_call(kernel, out_shape=jax.ShapeDtypeStruct(queries.shape, BF16...  72.6 us
    unnamed x3, local copies, waits for them, and re-layouts  2.71 us

profile of v6, /device:TPU:1, one launch (start us, length us, event | category | flops | bytes accessed | tf_op | source)
XLA Modules:
  0.0 76.1 jit_solution(17929763580746940485)
XLA Ops:
  0.0 0.0 copy-start
  0.0 0.7 copy-done
  0.7 0.1 reshape.7
  0.9 0.7 pad_add_fusion.ids_hbm
  1.5 72.6 %exchange_attend.1 = bf16[88,4096]{1,0:T(8,128)(2,1)} custom-call(s32[4,22]{1,0:T(4,128)} %pad_add_fusion.ids_hbm, bf16[8,8,896]{2,1,0:T(8,128)(2,1)} %db_ref.1, bf16[14,896]{1,0:T(8,128)(2,1)} %wsh_ref.1, bf16[88,4096]{1,0:T(8,128)(2,1)} %q_ref.1, bf16[896,512]{1,0:T(8,128)(2,1)} %wk_ref.1, bf16[896,512]{1,0:T(8,128)(2,1)} %wv_ref.1), custom_call_target="tpu_custom_call" | custom-call | tf_op jit(solution)/shard_map/exchange_attend/pallas_call | solution.py:451
  74.1 2.0 %copy.9 = bf16[88,4096]{1,0:T(8,128)(2,1)} copy(bf16[88,4096]{1,0:T(8,128)(2,1)} %exchange_attend.1) | data formatting | bytes 1441792
  (1 shorter events, 0.0 us)
Async XLA Ops:
  0.0 0.7 copy-start
